TPU v7x, 32 devices: a whole 2x2x4 slice. The times are simulated.
32 devices in a mesh: batch: 16 (over z, y, x), mp: 2 (over core).
Axes of the slice: x: 2, y: 2, z: 4, core: 2. Of those that a mesh axis runs over, the one named last changes fastest.
Arguments:
- hidden: bfloat16 [16384, 1024], P(('batch', 'mp')), may hold values from -6 to 6
- cell_ids: int32 [32, 512], P('batch'), may hold values from 0 to 127, never falling along the last dimension, each value on 1 to 60 neighbouring positions
- boxes: int32 [32, 128, 4], P('batch'), may hold values from 0 to 1023
- x_table: bfloat16 [1024, 1024], replicated, may hold values from -3 to 3
- y_table: bfloat16 [1024, 1024], replicated, may hold values from -3 to 3
- w_query: bfloat16 [1024, 1024], P(None, 'mp'), may hold values from -0.1875 to 0.1875
- b_query: bfloat16 [1024], P('mp'), may hold values from -3 to 3
- w_key: bfloat16 [1024, 1024], P(None, 'mp'), may hold values from -0.1875 to 0.1875
- w_value: bfloat16 [1024, 1024], P(None, 'mp'), may hold values from -0.1875 to 0.1875
- b_value: bfloat16 [1024], P('mp'), may hold values from -3 to 3
- w_out: bfloat16 [1024, 1024], P('mp'), may hold values from -3 to 3
- b_out: bfloat16 [1024], replicated, may hold values from -3 to 3
- ln1_gain: bfloat16 [1024], replicated, may hold values from 0.5 to 1.5
- ln1_bias: bfloat16 [1024], replicated, may hold values from -1 to 1
- w_up: bfloat16 [1024, 4096], P(None, 'mp'), may hold values from -0.1875 to 0.1875
- b_up: bfloat16 [4096], P('mp'), may hold values from -3 to 3
- w_down: bfloat16 [4096, 1024], P('mp'), may hold values from -0.09375 to 0.09375
- b_down: bfloat16 [1024], replicated, may hold values from -3 to 3
- ln2_gain: bfloat16 [1024], replicated, may hold values from 0.5 to 1.5
- ln2_bias: bfloat16 [1024], replicated, may hold values from -1 to 1
- d_out: bfloat16 [16384, 1024], P(('batch', 'mp')), may hold values from -6 to 6
Outputs:
- layer_out: bfloat16 [16384, 1024], P(('batch', 'mp'))
- d_hidden: float32 [16384, 1024], P(('batch', 'mp'))
- grad_w_query: float32 [1024, 1024], P(None, 'mp')
- grad_b_query: float32 [1024], P('mp')
- grad_w_key: float32 [1024, 1024], P(None, 'mp')
- grad_w_value: float32 [1024, 1024], P(None, 'mp')
- grad_b_value: float32 [1024], P('mp')
- grad_w_out: float32 [1024, 1024], P('mp')
- grad_b_out: float32 [1024], replicated
- grad_ln1_gain: float32 [1024], replicated
- grad_ln1_bias: float32 [1024], replicated
- grad_w_up: float32 [1024, 4096], P(None, 'mp')
- grad_b_up: float32 [4096], P('mp')
- grad_w_down: float32 [4096, 1024], P('mp')
- grad_b_down: float32 [1024], replicated
- grad_ln2_gain: float32 [1024], replicated
- grad_ln2_bias: float32 [1024], replicated
Inputs may be any that keep to these rules, and one draw needn't show every extreme that they name: `cell_ids`: numbered from 0 within each page, never falling along a page; each of the 128 cells has 1 to 60 tokens and one has 60.
All inputs are finite; a program needn't handle non-finite values.
Results may differ from a plain program's by a relative error of at most 0.023.
Values may be sent and summed in bfloat16 or wider, within the bound.
No kernel may reach another device: no remote copies, remote signals or barrier semaphores. Data moves between devices by JAX's collectives and lax.ppermute only.
A program may use at most 128 MiB of HBM per device.

v0:
```python
import functools

import jax
import jax.numpy as jnp
from jax import lax
from jax.experimental import pallas as pl
from jax.experimental.pallas import tpu as pltpu
from jax.sharding import PartitionSpec as P

HDIM = 64
PAGE_LEN = 512
CELLS = 128


def contract_rows(left, right):
    return lax.dot_general(
        left, right, (((0,), (0,)), ((), ())), preferred_element_type=jnp.float32
    )


def contract_last(left, right):
    return lax.dot_general(
        left, right, (((1,), (1,)), ((), ())), preferred_element_type=jnp.float32
    )


def layer_norm(values, gain, shift):
    average = jnp.mean(values, axis=-1, keepdims=True)
    centred = values - average
    rstd_rows = lax.rsqrt(jnp.mean(centred * centred, axis=-1, keepdims=True) + 1e-12)
    normed = centred * rstd_rows
    return (normed * gain + shift, normed, rstd_rows)


def norm_back(upstream, normed, rstd_rows, gain):
    scaled = upstream * gain
    return rstd_rows * (
        scaled
        - jnp.mean(scaled, axis=-1, keepdims=True)
        - normed * jnp.mean(scaled * normed, axis=-1, keepdims=True)
    )


def gelu_slope(values):
    return (
        0.5 * (1.0 + lax.erf(values * 0.7071067811865476))
        + values * jnp.exp(-0.5 * values * values) * 0.3989422804014327
    )


def page_scores(queries, keys_page):
    return jnp.einsum(
        "qhd,khd->hqk", queries, keys_page, preferred_element_type=jnp.float32
    ) * HDIM ** (-0.5)


def attend(page_block):
    queries, keys_page, values_page = page_block
    scores = page_scores(queries, keys_page)
    maximum = jnp.max(scores, axis=-1, keepdims=True)
    log_total = maximum + jnp.log(jnp.sum(jnp.exp(scores - maximum), axis=-1, keepdims=True))
    weights = jnp.exp(scores - log_total).astype(jnp.bfloat16)
    context = jnp.einsum("hqk,khd->qhd", weights, values_page, preferred_element_type=jnp.float32)
    return (context.astype(jnp.bfloat16), log_total[..., 0])


def attend_back(page_block):
    queries, keys_page, values_page, log_total, d_context = page_block
    weights = jnp.exp(page_scores(queries, keys_page) - log_total[..., None])
    d_weights = jnp.einsum(
        "qhd,khd->hqk", d_context, values_page, preferred_element_type=jnp.float32
    )
    d_values = jnp.einsum(
        "hqk,qhd->khd", weights.astype(jnp.bfloat16), d_context, preferred_element_type=jnp.float32
    )
    d_scores = (
        weights * (d_weights - jnp.sum(weights * d_weights, axis=-1, keepdims=True))
    ).astype(jnp.bfloat16)
    factor = HDIM ** (-0.5)
    d_queries = (
        jnp.einsum("hqk,khd->qhd", d_scores, keys_page, preferred_element_type=jnp.float32) * factor
    )
    d_keys = (
        jnp.einsum("hqk,qhd->khd", d_scores, queries, preferred_element_type=jnp.float32) * factor
    )
    return (
        d_queries.astype(jnp.bfloat16),
        d_keys.astype(jnp.bfloat16),
        d_values.astype(jnp.bfloat16),
    )


def shards_general(
    hidden,
    cell_ids,
    boxes,
    x_table,
    y_table,
    w_query,
    b_query,
    w_key,
    w_value,
    b_value,
    w_out,
    b_out,
    ln1_gain,
    ln1_bias,
    w_up,
    b_up,
    w_down,
    b_down,
    ln2_gain,
    ln2_bias,
    d_out,
):
    row_count = hidden.shape[0]
    width_local = w_query.shape[1]
    first_row = lax.axis_index("mp") * row_count
    own_cells = lax.dynamic_slice_in_dim(cell_ids.reshape(-1), first_row, row_count)
    page_local = (first_row + jnp.arange(row_count, dtype=jnp.int32)) // PAGE_LEN
    cell_boxes = jnp.take(boxes.reshape(-1, 4), page_local * CELLS + own_cells, axis=0)
    layout = (
        jnp.take(x_table, cell_boxes[:, 0], axis=0).astype(jnp.float32)
        + jnp.take(y_table, cell_boxes[:, 1], axis=0).astype(jnp.float32)
        + jnp.take(x_table, cell_boxes[:, 2], axis=0).astype(jnp.float32)
        + jnp.take(y_table, cell_boxes[:, 3], axis=0).astype(jnp.float32)
    )
    inputs = hidden.astype(jnp.float32) + layout
    x_all = lax.all_gather(inputs.astype(jnp.bfloat16), "mp", axis=0, tiled=True)
    queries = (
        jnp.dot(x_all, w_query, preferred_element_type=jnp.float32) + b_query.astype(jnp.float32)
    ).astype(jnp.bfloat16)
    keys_all = jnp.dot(x_all, w_key, preferred_element_type=jnp.float32).astype(jnp.bfloat16)
    values_all = (
        jnp.dot(x_all, w_value, preferred_element_type=jnp.float32) + b_value.astype(jnp.float32)
    ).astype(jnp.bfloat16)
    page_shape = (-1, PAGE_LEN, width_local // HDIM, HDIM)
    page_split = (
        queries.reshape(page_shape),
        keys_all.reshape(page_shape),
        values_all.reshape(page_shape),
    )
    context, log_total = lax.map(attend, page_split)
    context = context.reshape(-1, width_local)
    attn_rows = lax.psum_scatter(
        jnp.dot(context, w_out, preferred_element_type=jnp.float32),
        "mp",
        scatter_dimension=0,
        tiled=True,
    )
    resid = inputs + attn_rows + b_out.astype(jnp.float32)
    hidden_mid, normed_one, rstd_one = layer_norm(
        resid, ln1_gain.astype(jnp.float32), ln1_bias.astype(jnp.float32)
    )
    mid_low = hidden_mid.astype(jnp.bfloat16)
    mid_all = lax.all_gather(mid_low, "mp", axis=0, tiled=True)
    pre_act = jnp.dot(mid_all, w_up, preferred_element_type=jnp.float32) + b_up.astype(jnp.float32)
    activ = jax.nn.gelu(pre_act, approximate=False).astype(jnp.bfloat16)
    ffn_rows = lax.psum_scatter(
        jnp.dot(activ, w_down, preferred_element_type=jnp.float32),
        "mp",
        scatter_dimension=0,
        tiled=True,
    )
    second = hidden_mid + ffn_rows + b_down.astype(jnp.float32)
    final, normed_two, rstd_two = layer_norm(
        second, ln2_gain.astype(jnp.float32), ln2_bias.astype(jnp.float32)
    )
    layer_out = final.astype(jnp.bfloat16)
    upstream = d_out.astype(jnp.float32)
    grad_ln2_gain = jnp.sum(upstream * normed_two, axis=0)
    grad_ln2_bias = jnp.sum(upstream, axis=0)
    d_second = norm_back(upstream, normed_two, rstd_two, ln2_gain.astype(jnp.float32))
    grad_b_down = jnp.sum(d_second, axis=0)
    second_low = d_second.astype(jnp.bfloat16)
    grads_all = lax.all_gather(second_low, "mp", axis=0, tiled=True)
    grad_w_down = contract_rows(activ, grads_all)
    d_pre = (contract_last(grads_all, w_down) * gelu_slope(pre_act)).astype(jnp.bfloat16)
    grad_w_up = contract_rows(mid_all, d_pre)
    grad_b_up = jnp.sum(d_pre.astype(jnp.float32), axis=0)
    d_mid_ffn = lax.psum_scatter(contract_last(d_pre, w_up), "mp", scatter_dimension=0, tiled=True)
    d_mid = d_second + d_mid_ffn
    grad_ln1_gain = jnp.sum(d_mid * normed_one, axis=0)
    grad_ln1_bias = jnp.sum(d_mid, axis=0)
    d_resid = norm_back(d_mid, normed_one, rstd_one, ln1_gain.astype(jnp.float32))
    grad_b_out = jnp.sum(d_resid, axis=0)
    resid_all = lax.all_gather(d_resid.astype(jnp.bfloat16), "mp", axis=0, tiled=True)
    grad_w_out = contract_rows(context, resid_all)
    d_context = contract_last(resid_all, w_out).astype(jnp.bfloat16).reshape(page_shape)
    d_queries, d_keys, d_values = lax.map(attend_back, page_split + (log_total, d_context))
    d_queries = d_queries.reshape(-1, width_local)
    d_keys = d_keys.reshape(-1, width_local)
    d_values = d_values.reshape(-1, width_local)
    grad_w_query = contract_rows(x_all, d_queries)
    grad_w_key = contract_rows(x_all, d_keys)
    grad_w_value = contract_rows(x_all, d_values)
    grad_b_query = jnp.sum(d_queries.astype(jnp.float32), axis=0)
    grad_b_value = jnp.sum(d_values.astype(jnp.float32), axis=0)
    d_hidden = d_resid + lax.psum_scatter(
        (
            contract_last(d_queries, w_query)
            + contract_last(d_keys, w_key)
            + contract_last(d_values, w_value)
        ).astype(jnp.bfloat16),
        "mp",
        scatter_dimension=0,
        tiled=True,
    ).astype(jnp.float32)
    (
        grad_w_query,
        grad_b_query,
        grad_w_key,
        grad_w_value,
        grad_b_value,
        grad_w_out,
        grad_w_up,
        grad_b_up,
        grad_w_down,
    ) = (
        lax.psum(grad_w_query.astype(jnp.bfloat16), "batch").astype(jnp.float32),
        lax.psum(grad_b_query.astype(jnp.bfloat16), "batch").astype(jnp.float32),
        lax.psum(grad_w_key.astype(jnp.bfloat16), "batch").astype(jnp.float32),
        lax.psum(grad_w_value.astype(jnp.bfloat16), "batch").astype(jnp.float32),
        lax.psum(grad_b_value.astype(jnp.bfloat16), "batch").astype(jnp.float32),
        lax.psum(grad_w_out.astype(jnp.bfloat16), "batch").astype(jnp.float32),
        lax.psum(grad_w_up.astype(jnp.bfloat16), "batch").astype(jnp.float32),
        lax.psum(grad_b_up.astype(jnp.bfloat16), "batch").astype(jnp.float32),
        lax.psum(grad_w_down.astype(jnp.bfloat16), "batch").astype(jnp.float32),
    )
    grad_b_out, grad_ln1_gain, grad_ln1_bias, grad_b_down, grad_ln2_gain, grad_ln2_bias = lax.psum(
        (grad_b_out, grad_ln1_gain, grad_ln1_bias, grad_b_down, grad_ln2_gain, grad_ln2_bias),
        ("batch", "mp"),
    )
    return (
        layer_out,
        d_hidden,
        grad_w_query,
        grad_b_query,
        grad_w_key,
        grad_w_value,
        grad_b_value,
        grad_w_out,
        grad_b_out,
        grad_ln1_gain,
        grad_ln1_bias,
        grad_w_up,
        grad_b_up,
        grad_w_down,
        grad_b_down,
        grad_ln2_gain,
        grad_ln2_bias,
    )


def dot(left, right):
    return jnp.dot(left, right, preferred_element_type=jnp.float32)


def fixed(shape):
    return pl.BlockSpec(shape, lambda i: (0,) * len(shape))


LITTLE = pl.CostEstimate(flops=1, transcendentals=0, bytes_accessed=1)


def room(mebibytes):
    return pltpu.CompilerParams(vmem_limit_bytes=mebibytes * 2**20)


def stay(values):
    return pltpu.with_memory_space_constraint(values, pltpu.HBM)


def like(shape, kind=jnp.bfloat16):
    return jax.ShapeDtypeStruct(shape, kind)


def embed_kernel(
    page_ref, cells_ref, boxes_ref, x_ref, y_ref, hidden_ref, inputs_ref, low_ref, counts_ref, member_ref
):
    @pl.when(pl.program_id(0) == 0)
    def _():
        page = page_ref[0]
        boxes = boxes_ref[page]
        place = lax.broadcasted_iota(jnp.int32, counts_ref.shape[1:], 1)
        for j in range(2):
            counts = (place == boxes[:, j : j + 1]).astype(jnp.float32)
            counts = counts + (place == boxes[:, j + 2 : j + 3]).astype(jnp.float32)
            counts_ref[j] = counts.astype(jnp.bfloat16)
        ids = cells_ref[pl.ds(page, 1), :]
        member = lax.broadcasted_iota(jnp.int32, member_ref.shape, 0) == ids
        member_ref[...] = member.astype(jnp.float32).astype(jnp.bfloat16)

    cells = dot(counts_ref[0], x_ref[...]) + dot(counts_ref[1], y_ref[...])
    high = cells.astype(jnp.bfloat16)
    rest = cells - high.astype(jnp.float32)
    middle = rest.astype(jnp.bfloat16)
    low = (rest - middle.astype(jnp.float32)).astype(jnp.bfloat16)
    member = member_ref[...]
    layout = (
        contract_rows(member, high) + contract_rows(member, middle) + contract_rows(member, low)
    )
    inputs = hidden_ref[...].astype(jnp.float32) + layout
    inputs_ref[...] = inputs
    low_ref[...] = inputs.astype(jnp.bfloat16)


def embed(page, cell_ids, boxes, x_table, y_table, hidden):
    tokens, width = hidden.shape
    positions = x_table.shape[0]
    columns = 256
    return pl.pallas_call(
        embed_kernel,
        grid_spec=pltpu.PrefetchScalarGridSpec(
            num_scalar_prefetch=1,
            grid=(width // columns,),
            in_specs=[
                pl.BlockSpec(cell_ids.shape, lambda i, p: (0, 0)),
                pl.BlockSpec(boxes.shape, lambda i, p: (0, 0, 0)),
                pl.BlockSpec((positions, columns), lambda i, p: (0, i)),
                pl.BlockSpec((positions, columns), lambda i, p: (0, i)),
                pl.BlockSpec((tokens, columns), lambda i, p: (0, i)),
            ],
            out_specs=[
                pl.BlockSpec((tokens, columns), lambda i, p: (0, i)),
                pl.BlockSpec((tokens, columns), lambda i, p: (0, i)),
            ],
            scratch_shapes=[
                pltpu.VMEM((2, CELLS, positions), jnp.bfloat16),
                pltpu.VMEM((CELLS, tokens), jnp.bfloat16),
            ],
        ),
        out_shape=[like((tokens, width), jnp.float32), like((tokens, width))],
        cost_estimate=LITTLE,
        compiler_params=room(16),
        name="embed",
    )(page, cell_ids, boxes, x_table, y_table, hidden)


def pick(values, head):
    lanes = lax.broadcasted_iota(jnp.int32, values.shape, 1) // HDIM
    return jnp.where(lanes == head, values, jnp.zeros_like(values))


def attend_kernel(x_ref, wq_ref, wk_ref, wv_ref, b_ref, qkv_ref, context_ref, weights_ref):
    rows = 256
    pair = 2 * HDIM
    factor = HDIM ** (-0.5) * 1.4426950408889634
    x = x_ref[...]
    q = (dot(x, wq_ref[...]) + b_ref[0:1, :]).astype(jnp.bfloat16)
    k = dot(x, wk_ref[...]).astype(jnp.bfloat16)
    v = (dot(x, wv_ref[...]) + b_ref[1:2, :]).astype(jnp.bfloat16)
    qkv_ref[0] = q
    qkv_ref[1] = k
    qkv_ref[2] = v
    for start in range(0, x.shape[0], rows):
        here = slice(start, start + rows)
        for left in range(0, q.shape[1], pair):
            lanes = slice(left, left + pair)
            total = None
            for head in range(2):
                scores = contract_last(pick(q[here, lanes], head), k[:, lanes])
                maximum = jnp.max(scores, axis=-1, keepdims=True)
                powers = jnp.exp2((scores - maximum) * factor)
                weights = (powers * (1.0 / jnp.sum(powers, axis=-1, keepdims=True))).astype(
                    jnp.bfloat16
                )
                weights_ref[left // HDIM + head, here, :] = weights
                part = dot(weights, pick(v[:, lanes], head))
                total = part if total is None else total + part
            context_ref[here, lanes] = total.astype(jnp.bfloat16)


def attend_heads(x_low, w_query, w_key, w_value, biases):
    tokens, depth = x_low.shape
    width = w_query.shape[1]
    columns = 4 * HDIM
    weight = pl.BlockSpec((depth, columns), lambda i: (0, i))
    bias = pl.BlockSpec((biases.shape[0], columns), lambda i: (0, i))
    return pl.pallas_call(
        attend_kernel,
        grid=(width // columns,),
        in_specs=[fixed((tokens, depth)), weight, weight, weight, bias],
        out_specs=[
            pl.BlockSpec((3, tokens, columns), lambda i: (0, 0, i)),
            pl.BlockSpec((tokens, columns), lambda i: (0, i)),
            pl.BlockSpec((4, tokens, tokens), lambda i: (i, 0, 0)),
        ],
        out_shape=[
            like((3, tokens, width)),
            like((tokens, width)),
            pltpu.HBM((width // HDIM, tokens, tokens), jnp.bfloat16),
        ],
        cost_estimate=LITTLE,
        compiler_params=room(24),
        name="attend",
    )(x_low, w_query, w_key, w_value, biases)


def resid_kernel(
    inputs_ref, c0_ref, c1_ref, w0_ref, w1_ref, rows_ref, low_ref, normed_ref, rstd_ref
):
    resid = (
        inputs_ref[...]
        + (dot(c0_ref[...], w0_ref[...]) + dot(c1_ref[...], w1_ref[...]))
        + rows_ref[0:1, :]
    )
    mid, normed, rstd = layer_norm(resid, rows_ref[1:2, :], rows_ref[2:3, :])
    low_ref[...] = mid.astype(jnp.bfloat16)
    normed_ref[...] = normed
    rstd_ref[...] = rstd


def resid_norm(inputs, context, w_out, vectors):
    tokens, width = inputs.shape
    part = context[0].shape[1]
    rows = 128
    wide = pl.BlockSpec((rows, width), lambda i: (i, 0))
    half = pl.BlockSpec((rows, part), lambda i: (i, 0))
    weight = fixed((part, width))
    return pl.pallas_call(
        resid_kernel,
        grid=(tokens // rows,),
        in_specs=[wide, half, half, weight, weight, fixed(vectors.shape)],
        out_specs=[wide, wide, pl.BlockSpec((rows, 1), lambda i: (i, 0))],
        out_shape=[
            like((tokens, width)),
            like((tokens, width), jnp.float32),
            like((tokens, 1), jnp.float32),
        ],
        cost_estimate=LITTLE,
        compiler_params=room(16),
        name="resid_norm",
    )(inputs, *context, *w_out, vectors)


def up_kernel(mid_ref, w_ref, b_ref, activ_ref, slope_ref):
    rows = 128
    bias = b_ref[pl.ds(pl.program_id(0) + 2, 1), :]
    for start in range(0, mid_ref.shape[0], rows):
        here = slice(start, start + rows)
        pre = dot(mid_ref[here, :], w_ref[...]) + bias
        below = 0.5 * (1.0 + lax.erf(pre * 0.7071067811865476))
        density = jnp.exp(-0.5 * pre * pre) * 0.3989422804014327
        activ_ref[here, :] = (pre * below).astype(jnp.bfloat16)
        slope_ref[here, :] = (below + pre * density).astype(jnp.bfloat16)


def up(mid_low, w_up, biases):
    tokens, width = mid_low.shape
    units = w_up.shape[1]
    columns = biases.shape[1]
    out = pl.BlockSpec((tokens, columns), lambda i: (0, i))
    return pl.pallas_call(
        up_kernel,
        grid=(units // columns,),
        in_specs=[
            fixed((tokens, width)),
            pl.BlockSpec((width, columns), lambda i: (0, i)),
            fixed(biases.shape),
        ],
        out_specs=[out, out],
        out_shape=[like((tokens, units))] * 2,
        cost_estimate=LITTLE,
        compiler_params=room(16),
        name="up",
    )(mid_low, w_up, biases)


def column_sum(values):
    return jnp.sum(values, axis=0, keepdims=True)


def turn_kernel(
    a0_ref, a1_ref, w0_ref, w1_ref, normed_ref, rows_ref, d_out_ref,
    out_ref, d_second_ref, low_ref, sums_ref, acc_ref,
):
    step = pl.program_id(0)
    rows = out_ref.shape[0]
    sums_of = pl.num_programs(0) - acc_ref.shape[0] // rows

    def products():
        return dot(a0_ref[...], w0_ref[...]) + dot(a1_ref[...], w1_ref[...])

    @pl.when(step == 0)
    def _():
        acc_ref[...] = products()
        sums_ref[...] = jnp.zeros_like(sums_ref)

    @pl.when((step > 0) & (step < sums_of))
    def _():
        acc_ref[...] += products()

    @pl.when(step >= sums_of)
    def _():
        gain1, bias1, b_down, gain, bias = [rows_ref[j : j + 1, :] for j in range(1, 6)]
        first = (step - sums_of) * rows
        for start in range(0, rows, 64):
            here = slice(start, start + 64)
            acc = acc_ref[pl.ds(pl.multiple_of(first + start, 64), 64), :]
            second = normed_ref[here, :] * gain1 + bias1 + acc + b_down
            final, normed, rstd = layer_norm(second, gain, bias)
            out_ref[here, :] = final.astype(jnp.bfloat16)
            upstream = d_out_ref[here, :].astype(jnp.float32)
            d_second = norm_back(upstream, normed, rstd, gain)
            d_second_ref[here, :] = d_second
            low_ref[here, :] = d_second.astype(jnp.bfloat16)
            parts = (column_sum(upstream * normed), column_sum(upstream), column_sum(d_second))
            for j in range(3):
                sums_ref[j : j + 1, :] += parts[j]


def turn_back(activ, w_down, normed_one, vectors, d_out):
    tokens, units = activ[0].shape
    width = w_down[0].shape[1]
    columns, rows = 512, 128
    steps = units // columns
    wide = pl.BlockSpec((rows, width), lambda i: (jnp.maximum(i - steps, 0), 0))
    act = pl.BlockSpec((tokens, columns), lambda i: (0, jnp.minimum(i, steps - 1)))
    weight = pl.BlockSpec((columns, width), lambda i: (jnp.minimum(i, steps - 1), 0))
    return pl.pallas_call(
        turn_kernel,
        grid=(steps + tokens // rows,),
        in_specs=[act, act, weight, weight, wide, fixed(vectors.shape), wide],
        out_specs=[wide, wide, wide, fixed((8, width))],
        out_shape=[
            like((tokens, width)),
            like((tokens, width), jnp.float32),
            like((tokens, width)),
            like((8, width), jnp.float32),
        ],
        scratch_shapes=[pltpu.VMEM((tokens, width), jnp.float32)],
        cost_estimate=LITTLE,
        compiler_params=room(30),
        name="turn_back",
    )(*activ, *w_down, normed_one, vectors, d_out)


def grad_kernel(at_ref, left_ref, right_ref, *refs):
    right = right_ref[...] if len(right_ref.shape) == 2 else right_ref[0]
    out = contract_rows(left_ref[...], right)
    if len(refs) == 2:
        out = out + refs[0][...].astype(jnp.float32)
    refs[-1][...] = out.astype(jnp.bfloat16)


def weight_grad(at, left, right, start, rows, sent=None, which=None):
    tokens = left.shape[0]
    columns = right.shape[1]
    count = rows if which is None else rows // 2
    which = which or (lambda p: 0)
    take = min(count, 2**19 // columns)
    steps = count // take
    first = start // take
    assert start % take == 0 and count % take == 0
    return pl.pallas_call(
        grad_kernel,
        grid_spec=pltpu.PrefetchScalarGridSpec(
            num_scalar_prefetch=1,
            grid=(steps,),
            in_specs=[
                pl.BlockSpec((tokens, take), lambda i, p: (0, first + which(p) * steps + i)),
                pl.BlockSpec((tokens, columns), lambda i, p: (0, 0)),
            ]
            + [pl.BlockSpec((take, columns), lambda i, p: (first + which(p) * steps + i, 0))]
            * (sent is not None),
            out_specs=pl.BlockSpec((take, columns), lambda i, p: (i, 0)),
        ),
        out_shape=like((count, columns)),
        cost_estimate=LITTLE,
        compiler_params=room(12),
        name="weight_grad",
    )(at, left, right, *(() if sent is None else (sent,)))


def heads_grad(at, left, right, sent=None, which=None):
    tokens, rows = left.shape
    kinds, _, columns = right.shape
    count = rows if which is None else rows // 2
    parts = rows // count
    which = which or (lambda p: 0)
    return pl.pallas_call(
        grad_kernel,
        grid_spec=pltpu.PrefetchScalarGridSpec(
            num_scalar_prefetch=1,
            grid=(kinds,),
            in_specs=[
                pl.BlockSpec((tokens, count), lambda i, p: (0, which(p))),
                pl.BlockSpec((1, tokens, columns), lambda i, p: (i, 0, 0)),
            ]
            + [pl.BlockSpec((count, columns), lambda i, p: (i * parts + which(p), 0))]
            * (sent is not None),
            out_specs=pl.BlockSpec((count, columns), lambda i, p: (i, 0)),
        ),
        out_shape=like((kinds * count, columns)),
        cost_estimate=LITTLE,
        compiler_params=room(12),
        name="heads_grad",
    )(at, left, right, *(() if sent is None else (sent,)))


def combine_kernel(count, at_ref, *refs):
    terms = refs[:count]
    out = terms[0][...].astype(jnp.float32)
    for term in terms[1:]:
        out = out + term[...].astype(jnp.float32)
    refs[-1][...] = out.astype(refs[-1].dtype)


def combine(at, terms, rows, kind=jnp.bfloat16, slab=None, slabs=1, into=None):
    columns = terms[0][0].shape[1]
    blocks = 1
    while rows * columns // blocks > 2**19 or rows % blocks:
        blocks += 1
    take = rows // blocks
    slab = slab or (lambda p: 0)

    def spec(number):
        return pl.BlockSpec((take, columns), lambda i, p: (number(p) * blocks + i, 0))

    extra = [] if into is None else [into]
    return pl.pallas_call(
        functools.partial(combine_kernel, len(terms)),
        grid_spec=pltpu.PrefetchScalarGridSpec(
            num_scalar_prefetch=1,
            grid=(blocks,),
            in_specs=[spec(number) for _, number in terms]
            + [pl.BlockSpec(memory_space=pl.ANY) for _ in extra],
            out_specs=spec(slab),
        ),
        out_shape=like((rows * slabs, columns), kind),
        input_output_aliases={} if into is None else {1 + len(terms): 0},
        cost_estimate=LITTLE,
        compiler_params=room(10),
        name="combine",
    )(at, *[array for array, _ in terms], *extra)


def whole(p):
    return 0


def spread_kernel(count, at_ref, *refs):
    for j in range(count):
        refs[j - count][...] = refs[j][...].astype(jnp.float32)


def spread(at, values, count, slab, into):
    rows, columns = values.shape[0] // count, values.shape[1]
    extra = into or ()
    run = lambda j: pl.BlockSpec((rows, columns), lambda i, p: (j, 0))
    return pl.pallas_call(
        functools.partial(spread_kernel, count),
        grid_spec=pltpu.PrefetchScalarGridSpec(
            num_scalar_prefetch=1,
            grid=(1,),
            in_specs=[run(j) for j in range(count)]
            + [pl.BlockSpec(memory_space=pl.ANY) for _ in extra],
            out_specs=[pl.BlockSpec((rows, columns), lambda i, p: (slab(p), 0))] * count,
        ),
        out_shape=[like((2 * rows, columns), jnp.float32)] * count,
        input_output_aliases={1 + count + j: j for j in range(len(extra))},
        cost_estimate=LITTLE,
        compiler_params=room(16),
        name="spread",
    )(at, *[values] * count, *extra)


def pre_kernel(low_ref, w_ref, slope_ref, out_ref, sums_ref):
    d_pre = (contract_last(low_ref[...], w_ref[...]) * slope_ref[...].astype(jnp.float32)).astype(
        jnp.bfloat16
    )
    out_ref[...] = d_pre
    sums_ref[...] = column_sum(d_pre.astype(jnp.float32))


def pre_back(second_low, w_down, slope):
    tokens, width = second_low.shape
    units = w_down.shape[0]
    columns = 512
    out = pl.BlockSpec((tokens, columns), lambda i: (0, i))
    return pl.pallas_call(
        pre_kernel,
        grid=(units // columns,),
        in_specs=[fixed((tokens, width)), pl.BlockSpec((columns, width), lambda i: (i, 0)), out],
        out_specs=[out, pl.BlockSpec((1, columns), lambda i: (0, i))],
        out_shape=[like((tokens, units)), like((1, units), jnp.float32)],
        cost_estimate=LITTLE,
        compiler_params=room(14),
        name="pre_back",
    )(second_low, w_down, slope)


def mid_kernel(
    p0_ref, p1_ref, w0_ref, w1_ref, d_second_ref, normed_ref, rstd_ref, rows_ref,
    resid_ref, low_ref, sums_ref, acc_ref,
):
    step = pl.program_id(0)
    rows = low_ref.shape[0]
    sums_of = pl.num_programs(0) - acc_ref.shape[0] // rows

    def products():
        return contract_last(p0_ref[...], w0_ref[...]) + contract_last(p1_ref[...], w1_ref[...])

    @pl.when(step == 0)
    def _():
        acc_ref[...] = products()
        sums_ref[...] = jnp.zeros_like(sums_ref)

    @pl.when((step > 0) & (step < sums_of))
    def _():
        acc_ref[...] += products()

    @pl.when(step >= sums_of)
    def _():
        gain = rows_ref[1:2, :]
        first = (step - sums_of) * rows
        for start in range(0, rows, 64):
            here = slice(start, start + 64)
            acc = acc_ref[pl.ds(pl.multiple_of(first + start, 64), 64), :]
            d_mid = d_second_ref[here, :] + acc
            normed = normed_ref[here, :]
            d_resid = norm_back(d_mid, normed, rstd_ref[here, :], gain)
            resid_ref[here, :] = d_resid
            low_ref[here, :] = d_resid.astype(jnp.bfloat16)
            parts = (column_sum(d_resid), column_sum(d_mid * normed), column_sum(d_mid))
            for j in range(3):
                sums_ref[j : j + 1, :] += parts[j]


def mid_back(d_pre, w_up, d_second, normed, rstd, vectors):
    tokens, units = d_pre[0].shape
    width = w_up[0].shape[0]
    columns, rows = 512, 128
    steps = units // columns
    wide = pl.BlockSpec((rows, width), lambda i: (jnp.maximum(i - steps, 0), 0))
    part = pl.BlockSpec((tokens, columns), lambda i: (0, jnp.minimum(i, steps - 1)))
    weight = pl.BlockSpec((width, columns), lambda i: (0, jnp.minimum(i, steps - 1)))
    return pl.pallas_call(
        mid_kernel,
        grid=(steps + tokens // rows,),
        in_specs=[
            part, part, weight, weight, wide, wide,
            pl.BlockSpec((rows, 1), lambda i: (jnp.maximum(i - steps, 0), 0)), fixed(vectors.shape),
        ],
        out_specs=[wide, wide, fixed((8, width))],
        out_shape=[
            like((tokens, width), jnp.float32),
            like((tokens, width)),
            like((8, width), jnp.float32),
        ],
        scratch_shapes=[pltpu.VMEM((tokens, width), jnp.float32)],
        cost_estimate=LITTLE,
        compiler_params=room(30),
        name="mid_back",
    )(*d_pre, *w_up, d_second, normed, rstd, vectors)


def attend_back_kernel(qkv_ref, context_ref, weights_ref, low_ref, w_ref, out_ref, sums_ref):
    factor = HDIM ** (-0.5)
    queries, keys, values = qkv_ref[0], qkv_ref[1], qkv_ref[2]
    d_context = contract_last(low_ref[...], w_ref[...]).astype(jnp.bfloat16)
    product = d_context.astype(jnp.float32) * context_ref[...].astype(jnp.float32)
    grads = None
    for head in range(2):
        d_head = pick(d_context, head)
        d_weights = contract_last(d_head, values)
        inner = jnp.sum(pick(product, head), axis=-1, keepdims=True)
        weights = weights_ref[head]
        d_scores = (weights.astype(jnp.float32) * (d_weights - inner)).astype(jnp.bfloat16)
        parts = (
            dot(d_scores, pick(keys, head)),
            contract_rows(d_scores, pick(queries, head)),
            contract_rows(weights, d_head),
        )
        grads = parts if grads is None else tuple(a + b for a, b in zip(grads, parts))
    for j, scale in enumerate((factor, factor, 1.0)):
        grad = (grads[j] * scale).astype(jnp.bfloat16)
        out_ref[j] = grad
        sums_ref[j : j + 1, :] = column_sum(grad.astype(jnp.float32))


def attend_back_heads(qkv, context, weights, resid_low, w_out):
    _, tokens, width = qkv.shape
    depth = resid_low.shape[1]
    pair = 2 * HDIM
    block = pl.BlockSpec((3, tokens, pair), lambda i: (0, 0, i))
    return pl.pallas_call(
        attend_back_kernel,
        grid=(width // pair,),
        in_specs=[
            block,
            pl.BlockSpec((tokens, pair), lambda i: (0, i)),
            pl.BlockSpec((2, tokens, tokens), lambda i: (i, 0, 0)),
            fixed((tokens, depth)),
            pl.BlockSpec((pair, depth), lambda i: (i, 0)),
        ],
        out_specs=[block, pl.BlockSpec((8, pair), lambda i: (0, i))],
        out_shape=[like((3, tokens, width)), like((8, width), jnp.float32)],
        cost_estimate=LITTLE,
        compiler_params=room(16),
        name="attend_back",
    )(qkv, context, weights, resid_low, w_out)


def gather_kernel(h0_ref, h1_ref, p0_ref, p1_ref, mid_ref, second_ref, own_ref, other_ref):
    width = own_ref.shape[1]
    part = h0_ref.shape[1]
    for h_ref, p_ref, out_ref in ((h0_ref, p0_ref, own_ref), (h1_ref, p1_ref, other_ref)):
        out_ref[...] = jnp.zeros_like(out_ref)
        out_ref[0:1, :part] = h_ref[0:1, :]
        out_ref[0:1, part : 2 * part] = h_ref[2:3, :]
        for j in range(p_ref.shape[1] // width):
            out_ref[1 + j : 2 + j, :] = p_ref[:, j * width : (j + 1) * width]
        out_ref[8:11, :] = mid_ref[0:3, :]
        out_ref[11:14, :] = second_ref[0:3, :]


def gather_sums(heads, pre, mid, second):
    out = like((16, mid.shape[1]), jnp.float32)
    return pl.pallas_call(
        gather_kernel,
        out_shape=[out, out],
        cost_estimate=LITTLE,
        compiler_params=room(4),
        name="gather_sums",
    )(*heads, *pre, mid, second)


def last_kernel(d0_ref, d1_ref, *refs):
    resid_ref, out_ref = refs[6:]
    out = resid_ref[...]
    for j in range(3):
        out = out + (
            contract_last(d0_ref[j], refs[2 * j][...]) + contract_last(d1_ref[j], refs[2 * j + 1][...])
        )
    out_ref[...] = out


def last_back(d_heads, w_query, w_key, w_value, d_resid):
    tokens, width = d_resid.shape
    part = d_heads[0].shape[2]
    columns = 256
    heads = fixed((3, tokens, part))
    wide = pl.BlockSpec((tokens, columns), lambda i: (0, i))
    weight = pl.BlockSpec((columns, part), lambda i: (i, 0))
    return pl.pallas_call(
        last_kernel,
        grid=(width // columns,),
        in_specs=[heads, heads] + [weight] * 6 + [wide],
        out_specs=wide,
        out_shape=like((tokens, width), jnp.float32),
        cost_estimate=LITTLE,
        compiler_params=room(16),
        name="last_back",
    )(*d_heads, *w_query, *w_key, *w_value, d_resid)


def move(values, target):
    pairs = []
    for z in range(4):
        for y in range(2):
            for x in range(2):
                for core in range(2):
                    there = target(x, y, z, core)
                    if there is not None:
                        tx, ty, tz, tcore = there
                        pairs.append(
                            ((z * 4 + y * 2 + x) * 2 + core, (tz * 4 + ty * 2 + tx) * 2 + tcore)
                        )
    return lax.ppermute(values, ("batch", "mp"), pairs)


def swap_core(values):
    return move(values, lambda x, y, z, core: (x, y, z, 1 - core))


def turn(x, y, z, core, along):
    return (1 - x, y, z, core) if along == 0 else (x, 1 - y, z, core)


def swap_first(values):
    return move(values, lambda x, y, z, core: turn(x, y, z, core, core))


def swap_second(values):
    return move(values, lambda x, y, z, core: turn(x, y, z, core, 1 - core))


def swap_near(values):
    return move(values, lambda x, y, z, core: (x, y, z ^ 1, core))


def swap_far(values):
    return move(values, lambda x, y, z, core: (x, y, 3 - z, core))


def placement():
    batch, core = lax.axis_index("batch"), lax.axis_index("mp")
    x, y, z = batch % 2, batch // 2 % 2, batch // 4
    first, second = jnp.where(core == 0, x, y), jnp.where(core == 0, y, x)
    near = jnp.where((z == 1) | (z == 2), 1, 0)
    return jnp.stack([first, second, near, z // 2, core]).astype(jnp.int32)


PLANE_FIRST = ((0, swap_first), (1, swap_second), (2, swap_near), (3, swap_far))
LINE_FIRST = ((2, swap_near), (3, swap_far), (0, swap_first), (1, swap_second))


ORDER = (
    "down", "pre", "up", "D", "pre", "mid", "out", "U", "O", "D", "D", "attn", "O", "O",
    "heads", "U", "U", "attn", "small", "U", "O", "H", "H", "U", "D", "O", "small", "U",
    "H", "D", "U", "H", "U", "O", "small", "small", "H", "O", "D", "D", "H", "H", "D",
    "U", "H", "small", "small", "O", "last", "D", "O", "H",
)


class Line:
    def __init__(self):
        self.last = ()

    def after(self, *values):
        tied = lax.optimization_barrier((values, self.last))[0]
        return tied[0] if len(values) == 1 else tied

    def did(self, *results):
        self.last = results
        return results[0] if len(results) == 1 else results


def sum_chips(line, at, order, make, finish):
    (a, move_a), (b, move_b), (c, move_c), (_, move_d) = order
    mine = lambda k: lambda p: p[k]
    theirs = lambda k: lambda p: 1 - p[k]
    got_a = move_a(make(theirs(a)))
    yield
    half = make(mine(a))
    yield
    half, got_a = line.after(half, got_a)
    rows = half.shape[0] // 2
    got_b = move_b(line.did(combine(at, [(half, theirs(b)), (got_a, theirs(b))], rows)))
    yield
    got_b = line.after(got_b)
    rows //= 2
    there = lambda p: 2 * p[b] + 1 - p[c]
    here = lambda p: 2 * p[b] + p[c]
    got_c = move_c(line.did(combine(at, [(half, there), (got_a, there), (got_b, theirs(c))], rows)))
    yield
    got_c = line.after(got_c)
    part = line.did(combine(at, [(half, here), (got_a, here), (got_b, mine(c)), (got_c, whole)], rows))
    got_d = move_d(part)
    yield
    part, got_d = line.after(part, got_d)
    part = line.did(combine(at, [(part, whole), (got_d, whole)], rows))
    got_c = move_c(part)
    quarter = line.did(combine(at, [(part, whole)], rows, slab=mine(c), slabs=2))
    yield
    quarter, got_c = line.after(quarter, got_c)
    quarter = line.did(combine(at, [(got_c, whole)], rows, slab=theirs(c), slabs=2, into=quarter))
    got_b = move_b(quarter)
    half = line.did(combine(at, [(quarter, whole)], 2 * rows, slab=mine(b), slabs=2))
    yield
    half, got_b = line.after(half, got_b)
    half = line.did(combine(at, [(got_b, whole)], 2 * rows, slab=theirs(b), slabs=2, into=half))
    got_a = move_a(half)
    out = line.did(finish(half, mine(a), None))
    yield
    got_a = line.after(got_a)
    line.did(finish(got_a, theirs(a), out))
    yield


def sum_small(line, values):
    for move_on in (swap_first, swap_second, swap_near, swap_far):
        values = line.did(line.after(values))
        got = move_on(values)
        yield
        values, got = line.after(values, got)
        values = line.did(values + got)
    return values


def shards_paged(
    hidden,
    cell_ids,
    boxes,
    x_table,
    y_table,
    w_query,
    b_query,
    w_key,
    w_value,
    b_value,
    w_out,
    b_out,
    ln1_gain,
    ln1_bias,
    w_up,
    b_up,
    w_down,
    b_down,
    ln2_gain,
    ln2_bias,
    d_out,
):
    at = placement()
    page = lax.axis_index("mp").reshape(1)
    line = Line()
    split = jnp.concatenate([b_query, b_value, b_up])
    part = b_query.shape[0]
    split = (split, line.did(swap_core(split)))
    hidden = line.after(hidden)
    split = [v.astype(jnp.float32).reshape(-1, part) for v in split]
    rows = jnp.concatenate([b_out, ln1_gain, ln1_bias, b_down, ln2_gain, ln2_bias])
    rows = rows.astype(jnp.float32).reshape(6, -1)
    x_table, y_table, hidden, d_out = [stay(v) for v in (x_table, y_table, hidden, d_out)]
    w_query, w_key, w_value = [(stay(w), stay(swap_core(w))) for w in (w_query, w_key, w_value)]
    both = (0, 1)

    inputs, x_low = embed(page, cell_ids, boxes, x_table, y_table, hidden)
    attended = [attend_heads(x_low, w_query[i], w_key[i], w_value[i], split[i]) for i in both]
    qkv, context, weights = zip(*attended)
    line.did(x_low, w_query[1], w_key[1], w_value[1])
    w_out, w_up, w_down = [
        (stay(w), stay(swap_core(line.after(w)))) for w in (w_out, w_up, w_down)
    ]
    mid_low, normed_one, rstd_one = resid_norm(inputs, context, w_out, rows)
    activ, slope = zip(*[up(mid_low, w_up[i], split[i]) for i in both])
    layer_out, d_second, second_low, second_sums = turn_back(
        activ, w_down, normed_one, rows, d_out
    )
    line.did(second_low)
    found = {"d_pre": {}, "pre sums": {}, "heads": {}, "heads sums": {}}

    def grads(name, product, left, right):
        found[name] = swap_core(line.did(product(line.after(left(1)), right(1))))
        yield

    def halves(name, product, left, right):
        def make(which):
            mine, sent = line.after(left(0), found[name])
            return line.did(product(mine, right(0), sent, which))

        return make

    def pre_steps():
        for i in (1, 0):
            low = line.after(second_low)
            found["d_pre"][i], found["pre sums"][i] = pre_back(low, w_down[i], slope[i])
            line.did(found["d_pre"][i])
            yield

    def mid_steps():
        d_pre = [found["d_pre"][i] for i in both]
        d_pre[0] = line.after(d_pre[0])
        found["d_resid"], found["resid_low"], found["mid sums"] = mid_back(
            d_pre, w_up, d_second, normed_one, rstd_one, rows
        )
        line.did(found["resid_low"])
        yield

    def attend_steps():
        for i in (1, 0):
            low = line.after(found["resid_low"])
            found["heads"][i], found["heads sums"][i] = attend_back_heads(
                qkv[i], context[i], weights[i], low, w_out[i]
            )
            line.did(found["heads"][i])
            yield

    def last_steps():
        d_heads = [found["heads"][i] for i in both]
        d_heads[0] = line.after(d_heads[0])
        found["d_hidden"] = line.did(
            last_back(d_heads, w_query, w_key, w_value, found["d_resid"])
        )
        yield

    def small_steps():
        own, other = line.did(
            gather_sums(
                [line.after(found["heads sums"][i]) for i in both],
                [found["pre sums"][i] for i in both],
                found["mid sums"],
                second_sums,
            )
        )
        got = swap_core(other)
        yield
        own, got = line.after(own, got)
        found["small"] = yield from sum_small(line, own + got)
        line.did(found["small"])
        yield

    def store(name):
        def finish(values, slab, into):
            rows = values.shape[0]
            found[name] = combine(
                at, [(values, whole)], rows, kind=jnp.float32, slab=slab, slabs=2, into=into
            )
            return found[name]

        return finish

    def store_heads(values, slab, into):
        found["heads grads"] = tuple(spread(at, values, 3, slab, into))
        return found["heads grads"]

    units, depth = activ[0].shape[1], mid_low.shape[1]
    second_of = lambda i: second_low
    mid_of = lambda i: mid_low
    pre_of = lambda i: found["d_pre"][i]
    resid_of = lambda i: found["resid_low"]
    activ_of = lambda i: activ[i]
    context_of = lambda i: context[i]
    x_of = lambda i: x_low
    heads_of = lambda i: found["heads"][i]

    def span(start, rows):
        def product(left, right, sent=None, which=None):
            return weight_grad(at, left, right, start, rows, sent, which)

        return product

    def heads_product(left, right, sent=None, which=None):
        return heads_grad(at, left, right, sent, which)

    cut = depth * 3 // 4
    steps = {
        "down": grads("down", span(0, units), activ_of, second_of),
        "pre": pre_steps(),
        "up": grads("up", span(0, depth), mid_of, pre_of),
        "mid": mid_steps(),
        "out": grads("out", span(0, context[0].shape[1]), context_of, resid_of),
        "attn": attend_steps(),
        "heads": grads("qkv", heads_product, x_of, heads_of),
        "last": last_steps(),
        "small": small_steps(),
    }
    chunks = {
        "D": (PLANE_FIRST, lambda: halves("down", span(0, units), activ_of, second_of), store("grad down")),
        "U": (PLANE_FIRST, lambda: halves("up", span(0, depth), mid_of, pre_of), store("grad up")),
        "O": (LINE_FIRST, lambda: halves("out", span(0, context[0].shape[1]), context_of, resid_of), store("grad out")),
        "H": (PLANE_FIRST, lambda: halves("qkv", heads_product, x_of, heads_of), store_heads),
    }
    for name in ORDER:
        if name not in steps:
            order, make, finish = chunks[name]
            steps[name] = sum_chips(line, at, order, make(), finish)
        next(steps[name])
    d_hidden = found["d_hidden"]
    grad_w_down, grad_w_up, grad_w_out = [found["grad " + n] for n in ("down", "up", "out")]
    grad_w_query, grad_w_key, grad_w_value = found["heads grads"]
    small = found["small"]
    grad_b_query, grad_b_value = small[0, :part], small[0, part : 2 * part]
    grad_b_up = small[1 : 1 + units // depth].reshape(-1)
    grad_b_out, grad_ln1_gain, grad_ln1_bias, grad_ln2_gain, grad_ln2_bias, grad_b_down = [
        small[j] for j in range(8, 14)
    ]
    return (
        layer_out,
        d_hidden,
        grad_w_query,
        grad_b_query,
        grad_w_key,
        grad_w_value,
        grad_b_value,
        grad_w_out,
        grad_b_out,
        grad_ln1_gain,
        grad_ln1_bias,
        grad_w_up,
        grad_b_up,
        grad_w_down,
        grad_b_down,
        grad_ln2_gain,
        grad_ln2_bias,
    )


def solution(mesh):
    in_specs = (
        P(("batch", "mp"), None),
        P("batch", None),
        P("batch", None, None),
        P(),
        P(),
        P(None, "mp"),
        P("mp"),
        P(None, "mp"),
        P(None, "mp"),
        P("mp"),
        P("mp", None),
        P(),
        P(),
        P(),
        P(None, "mp"),
        P("mp"),
        P("mp", None),
        P(),
        P(),
        P(),
        P(("batch", "mp"), None),
    )
    out_specs = (
        P(("batch", "mp"), None),
        P(("batch", "mp"), None),
        P(None, "mp"),
        P("mp"),
        P(None, "mp"),
        P(None, "mp"),
        P("mp"),
        P("mp", None),
        P(),
        P(),
        P(),
        P(None, "mp"),
        P("mp"),
        P("mp", None),
        P(),
        P(),
        P(),
    )
    paged = mesh.shape["mp"] == 2 and mesh.shape["batch"] == 16
    shards = shards_paged if paged else shards_general
    return jax.shard_map(shards, mesh=mesh, in_specs=in_specs, out_specs=out_specs, check_vma=False)
```

profile of v0, /device:TPU:0, one launch (start us, length us, event | category | flops | bytes accessed | tf_op | source)
XLA Modules:
  0.0 324.6 jit_solution(8244780973261600048)
XLA Ops:
  7.1 5.9 %embed.1 = (f32[512,1024]{1,0:T(8,128)S(1)}, bf16[512,1024]{1,0:T(8,128)(2,1)S(1)}) custom-call(s32[1]{0:T(128)} %bitcast.page_ref, s32[2,512]{1,0:T(2,128)S(1)} %copy-done.6, s32[2,128,4]{2,1,0:T(8,128)S(1)} %copy.52.boxes_ref, bf16[1024,1024]{1,0:T(8,128)(2,1)} %x_ref.1, bf16[1024,1024]{1,0:T(8,128)(2,1)} %y_ref.1, bf16[512,1024]{1,0:T(8,128)(2,1)} %hidden_ref), custom_call_target="tpu_custom_call" | custom-call | flops 1 | bytes 1 | tf_op jit(solution)/shard_map/embed/pallas_call | solution.py:312
  14.2 9.9 %attend.2 = (bf16[3,512,512]{2,1,0:T(8,128)(2,1)S(1)}, bf16[512,512]{1,0:T(8,128)(2,1)S(1)}, bf16[8,512,512]{2,1,0:T(8,128)(2,1)}) custom-call(bf16[512,1024]{1,0:T(8,128)(2,1)S(1)} %get-tuple-element.210.x_ref.left_ref, bf16[1024,512]{1,0:T(8,128)(2,1)} %refs_0_.1, bf16[1024,512]{1,0:T(8,128)(2,1)} %refs_2_.1, bf16[1024,512]{1,0:T(8,128)(2,1)} %refs_4_.1, ...), custom_call_target="tpu_custom_call" | custom-call | flops 1 | bytes 1 | tf_op jit(solution)/shard_map/attend/pallas_call | solution.py:380
  24.1 10.5 %attend.3 = (bf16[3,512,512]{2,1,0:T(8,128)(2,1)S(1)}, bf16[512,512]{1,0:T(8,128)(2,1)S(1)}, bf16[8,512,512]{2,1,0:T(8,128)(2,1)}) custom-call(bf16[512,1024]{1,0:T(8,128)(2,1)S(1)} %get-tuple-element.210.x_ref.left_ref, bf16[1024,512]{1,0:T(8,128)(2,1)} %collective-permute-done.1.wq_ref.refs_1_, bf16[1024,512]{1,0:T(8,128)(2,1)} %collective-permute-done.2.wk_ref.refs_3_, ...), custom_call_target="tpu_custom_call" | custom-call | flops 1 | bytes 1 | tf_op jit(solution)/shard_map/attend/pallas_call | solution.py:380
  34.6 4.9 %resid_norm.1 = (bf16[512,1024]{1,0:T(8,128)(2,1)S(1)}, f32[512,1024]{1,0:T(8,128)S(1)}, f32[512,1]{1,0:T(8,128)S(1)}) custom-call(f32[512,1024]{1,0:T(8,128)S(1)} %get-tuple-element.143.inputs_ref, bf16[512,512]{1,0:T(8,128)(2,1)S(1)} %get-tuple-element.185.c0_ref.left_ref.context_ref, bf16[512,512]{1,0:T(8,128)(2,1)S(1)} %get-tuple-element.172.c1_ref.left_ref.context_ref, ...), custom_call_target="tpu_custom_call" | custom-call | flops 1 | bytes 1 | tf_op jit(solution)/shard_map/resid_norm/pallas_call | solution.py:421
  39.5 5.9 %up.2 = (bf16[512,2048]{1,0:T(8,128)(2,1)S(1)}, bf16[512,2048]{1,0:T(8,128)(2,1)S(1)}) custom-call(bf16[512,1024]{1,0:T(8,128)(2,1)S(1)} %get-tuple-element.190.mid_ref.left_ref, bf16[1024,2048]{1,0:T(8,128)(2,1)} %w0_ref.5, f32[6,512]{1,0:T(8,128)S(1)} %reshape.57.b_ref), custom_call_target="tpu_custom_call" | custom-call | flops 1 | bytes 1 | tf_op jit(solution)/shard_map/up/pallas_call | solution.py:454
  45.4 5.9 %up.3 = (bf16[512,2048]{1,0:T(8,128)(2,1)S(1)}, bf16[512,2048]{1,0:T(8,128)(2,1)S(1)}) custom-call(bf16[512,1024]{1,0:T(8,128)(2,1)S(1)} %get-tuple-element.190.mid_ref.left_ref, bf16[1024,2048]{1,0:T(8,128)(2,1)} %collective-permute-done.5.w_ref.w1_ref, f32[6,512]{1,0:T(8,128)S(1)} %reshape.59.b_ref), custom_call_target="tpu_custom_call" | custom-call | flops 1 | bytes 1 | tf_op jit(solution)/shard_map/up/pallas_call | solution.py:454
  51.3 11.3 %turn_back.1 = (bf16[512,1024]{1,0:T(8,128)(2,1)}, f32[512,1024]{1,0:T(8,128)S(1)}, bf16[512,1024]{1,0:T(8,128)(2,1)S(1)}, f32[8,1024]{1,0:T(8,128)S(1)}) custom-call(bf16[512,2048]{1,0:T(8,128)(2,1)S(1)} %get-tuple-element.179.a0_ref.left_ref, bf16[512,2048]{1,0:T(8,128)(2,1)S(1)} %get-tuple-element.158.a1_ref.left_ref, bf16[2048,1024]{1,0:T(8,128)(2,1)} %w_ref.4, ...), custom_call_target="tpu_custom_call" | custom-call | flops 1 | bytes 1 | tf_op jit(solution)/shard_map/turn_back/pallas_call | solution.py:521
  62.7 3.7 %weight_grad.9 = bf16[2048,1024]{1,0:T(8,128)(2,1)S(1)} custom-call(s32[5]{0:T(128)S(1)} %stack.20.at_ref, bf16[512,2048]{1,0:T(8,128)(2,1)S(1)} %get-tuple-element.158.a1_ref.left_ref, bf16[512,1024]{1,0:T(8,128)(2,1)S(1)} %get-tuple-element.165.right_ref.low_ref), custom_call_target="tpu_custom_call" | custom-call | flops 1 | bytes 1 | tf_op jit(solution)/shard_map/weight_grad/pallas_call | solution.py:556
  66.8 5.0 %pre_back.2 = (bf16[512,2048]{1,0:T(8,128)(2,1)S(1)}, f32[1,2048]{1,0:T(1,128)S(1)}) custom-call(bf16[512,1024]{1,0:T(8,128)(2,1)S(1)} %get-tuple-element.165.right_ref.low_ref, bf16[2048,1024]{1,0:T(8,128)(2,1)} %collective-permute-done.6.w1_ref.w_ref, bf16[512,2048]{1,0:T(8,128)(2,1)S(1)} %get-tuple-element.160.slope_ref), custom_call_target="tpu_custom_call" | custom-call | flops 1 | bytes 1 | tf_op jit(solution)/shard_map/pre_back/pallas_call | solution.py:682
  71.9 4.9 %weight_grad.10 = bf16[1024,2048]{1,0:T(8,128)(2,1)} custom-call(s32[5]{0:T(128)S(1)} %stack.20.at_ref, bf16[512,1024]{1,0:T(8,128)(2,1)S(1)} %get-tuple-element.190.mid_ref.left_ref, bf16[512,2048]{1,0:T(8,128)(2,1)S(1)} %get-tuple-element.161.right_ref.p1_ref), custom_call_target="tpu_custom_call" | custom-call | flops 1 | bytes 1 | tf_op jit(solution)/shard_map/weight_grad/pallas_call | solution.py:556
  82.0 5.0 %pre_back.3 = (bf16[512,2048]{1,0:T(8,128)(2,1)S(1)}, f32[1,2048]{1,0:T(1,128)S(1)}) custom-call(bf16[512,1024]{1,0:T(8,128)(2,1)S(1)} %get-tuple-element.165.right_ref.low_ref, bf16[2048,1024]{1,0:T(8,128)(2,1)} %w_ref.4, bf16[512,2048]{1,0:T(8,128)(2,1)S(1)} %get-tuple-element.166.slope_ref), custom_call_target="tpu_custom_call" | custom-call | flops 1 | bytes 1 | tf_op jit(solution)/shard_map/pre_back/pallas_call | solution.py:682
  87.0 8.9 %mid_back.1 = (f32[512,1024]{1,0:T(8,128)S(1)}, bf16[512,1024]{1,0:T(8,128)(2,1)S(1)}, f32[8,1024]{1,0:T(8,128)S(1)}) custom-call(bf16[512,2048]{1,0:T(8,128)(2,1)S(1)} %get-tuple-element.168.p0_ref.right_ref, bf16[512,2048]{1,0:T(8,128)(2,1)S(1)} %get-tuple-element.161.right_ref.p1_ref, bf16[1024,2048]{1,0:T(8,128)(2,1)} %w0_ref.5, ...), custom_call_target="tpu_custom_call" | custom-call | flops 1 | bytes 1 | tf_op jit(solution)/shard_map/mid_back/pallas_call | solution.py:739
  108.0 9.5 %attend_back.2 = (bf16[3,512,512]{2,1,0:T(8,128)(2,1)S(1)}, f32[8,512]{1,0:T(8,128)S(1)}) custom-call(bf16[3,512,512]{2,1,0:T(8,128)(2,1)S(1)} %copy-done.5, bf16[512,512]{1,0:T(8,128)(2,1)S(1)} %get-tuple-element.172.c1_ref.left_ref.context_ref, bf16[8,512,512]{2,1,0:T(8,128)(2,1)S(1)} %copy-done.1, ...), custom_call_target="tpu_custom_call" | custom-call | flops 1 | bytes 1 | tf_op jit(solution)/shard_map/attend_back/pallas_call | solution.py:788
  124.3 4.4 %collective-permute-done.12.refs_1_ = bf16[512,2048]{1,0:T(8,128)(2,1)S(1)} collective-permute-done((bf16[512,2048]{1,0:T(8,128)(2,1)S(1)}, bf16[512,2048]{1,0:T(8,128)(2,1)S(1)}, u32[]{:S(2)}, u32[]{:S(2)}) %collective-permute-start.12) | collective-permute-done | bytes 2097184 | tf_op jit(solution)/shard_map/ppermute | solution.py:871
  131.4 3.6 %collective-permute-start.13 = (bf16[128,1024]{1,0:T(8,128)(2,1)S(1)}, bf16[128,1024]{1,0:T(8,128)(2,1)S(1)}, u32[]{:S(2)}, u32[]{:S(2)}) collective-permute-start(bf16[128,1024]{1,0:T(8,128)(2,1)S(1)} %combine.39), channel_id=1, source_target_pairs={{0,24},{1,25},{2,26},{3,27},{4,28},{5,29},{6,30},{7,31},{8,16},{9,... | collective-permute-start | bytes 786440 | tf_op jit(solution)/shard_map/ppermute | solution.py:871
  135.5 9.3 %attend_back.3 = (bf16[3,512,512]{2,1,0:T(8,128)(2,1)S(1)}, f32[8,512]{1,0:T(8,128)S(1)}) custom-call(bf16[3,512,512]{2,1,0:T(8,128)(2,1)S(1)} %copy-done.3, bf16[512,512]{1,0:T(8,128)(2,1)S(1)} %get-tuple-element.185.c0_ref.left_ref.context_ref, bf16[8,512,512]{2,1,0:T(8,128)(2,1)S(1)} %copy-done, ...), custom_call_target="tpu_custom_call" | custom-call | flops 1 | bytes 1 | tf_op jit(solution)/shard_map/attend_back/pallas_call | solution.py:788
  153.3 4.6 %collective-permute-done.17.refs_3_ = bf16[128,2048]{1,0:T(8,128)(2,1)S(1)} collective-permute-done((bf16[128,2048]{1,0:T(8,128)(2,1)S(1)}, bf16[128,2048]{1,0:T(8,128)(2,1)S(1)}, u32[]{:S(2)}, u32[]{:S(2)}) %collective-permute-start.17) | collective-permute-done | bytes 524320 | tf_op jit(solution)/shard_map/ppermute | solution.py:871
  158.8 3.4 %collective-permute-start.20 = (bf16[128,2048]{1,0:T(8,128)(2,1)S(1)}, bf16[128,2048]{1,0:T(8,128)(2,1)S(1)}, u32[]{:S(2)}, u32[]{:S(2)}) collective-permute-start(bf16[128,2048]{1,0:T(8,128)(2,1)S(1)} %combine.43.refs_0_), channel_id=1, source_target_pairs={{0,24},{1,25},{2,26},{3,27},{4,28},{5,29},{6,30},{7,31},{8,16},{9,... | collective-permute-start | bytes 1572872 | tf_op jit(solution)/shard_map/ppermute | solution.py:871
  164.5 7.7 %collective-permute-done.15.refs_3_ = bf16[64,1024]{1,0:T(8,128)(2,1)S(1)} collective-permute-done((bf16[64,1024]{1,0:T(8,128)(2,1)S(1)}, bf16[64,1024]{1,0:T(8,128)(2,1)S(1)}, u32[]{:S(2)}, u32[]{:S(2)}) %collective-permute-start.15) | collective-permute-done | bytes 131104 | tf_op jit(solution)/shard_map/ppermute | solution.py:871
  176.1 7.3 %collective-permute-start.22 = (bf16[128,2048]{1,0:T(8,128)(2,1)S(1)}, bf16[128,2048]{1,0:T(8,128)(2,1)S(1)}, u32[]{:S(2)}, u32[]{:S(2)}) collective-permute-start(bf16[128,2048]{1,0:T(8,128)(2,1)S(1)} %combine.46.refs_0_), channel_id=1, source_target_pairs={{0,8},{1,9},{2,10},{3,11},{4,12},{5,13},{6,14},{7,15},{8,0},{9,1},... | collective-permute-start | bytes 1572872 | tf_op jit(solution)/shard_map/ppermute | solution.py:871
  185.6 8.9 %collective-permute-done.22.refs_0_ = bf16[128,2048]{1,0:T(8,128)(2,1)S(1)} collective-permute-done((bf16[128,2048]{1,0:T(8,128)(2,1)S(1)}, bf16[128,2048]{1,0:T(8,128)(2,1)S(1)}, u32[]{:S(2)}, u32[]{:S(2)}) %collective-permute-start.22) | collective-permute-done | bytes 524320 | tf_op jit(solution)/shard_map/ppermute | solution.py:871
  197.2 3.4 %collective-permute-start.34 = (bf16[256,1024]{1,0:T(8,128)(2,1)S(1)}, bf16[256,1024]{1,0:T(8,128)(2,1)S(1)}, u32[]{:S(2)}, u32[]{:S(2)}) collective-permute-start(bf16[256,1024]{1,0:T(8,128)(2,1)S(1)} %combine.49.refs_0_), channel_id=1, source_target_pairs={{0,24},{1,25},{2,26},{3,27},{4,28},{5,29},{6,30},{7,31},{8,16},{9,... | collective-permute-start | bytes 1572872 | tf_op jit(solution)/shard_map/ppermute | solution.py:871
  201.2 17.2 %collective-permute-done.26.refs_2_ = bf16[768,512]{1,0:T(8,128)(2,1)S(1)} collective-permute-done((bf16[768,512]{1,0:T(8,128)(2,1)S(1)}, bf16[768,512]{1,0:T(8,128)(2,1)S(1)}, u32[]{:S(2)}, u32[]{:S(2)}) %collective-permute-start.26) | collective-permute-done | bytes 786464 | tf_op jit(solution)/shard_map/ppermute | solution.py:871
  237.9 3.3 %collective-permute-start.33 = (bf16[384,512]{1,0:T(8,128)(2,1)S(1)}, bf16[384,512]{1,0:T(8,128)(2,1)S(1)}, u32[]{:S(2)}, u32[]{:S(2)}) collective-permute-start(bf16[384,512]{1,0:T(8,128)(2,1)S(1)} %combine.57.refs_0_), channel_id=1, source_target_pairs={{0,24},{1,25},{2,26},{3,27},{4,28},{5,29},{6,30},{7,31},{8,16},{9,... | collective-permute-start | bytes 1179656 | tf_op jit(solution)/shard_map/ppermute | solution.py:871
  241.8 6.4 %collective-permute-done.35.refs_0_ = bf16[256,1024]{1,0:T(8,128)(2,1)S(1)} collective-permute-done((bf16[256,1024]{1,0:T(8,128)(2,1)S(1)}, bf16[256,1024]{1,0:T(8,128)(2,1)S(1)}, u32[]{:S(2)}, u32[]{:S(2)}) %collective-permute-start.35) | collective-permute-done | bytes 524320 | tf_op jit(solution)/shard_map/ppermute | solution.py:871
  251.6 8.1 %collective-permute-done.33.refs_1_ = bf16[384,512]{1,0:T(8,128)(2,1)S(1)} collective-permute-done((bf16[384,512]{1,0:T(8,128)(2,1)S(1)}, bf16[384,512]{1,0:T(8,128)(2,1)S(1)}, u32[]{:S(2)}, u32[]{:S(2)}) %collective-permute-start.33) | collective-permute-done | bytes 393248 | tf_op jit(solution)/shard_map/ppermute | solution.py:871
  261.0 7.2 %collective-permute-done.36.refs_0_ = bf16[384,512]{1,0:T(8,128)(2,1)S(1)} collective-permute-done((bf16[384,512]{1,0:T(8,128)(2,1)S(1)}, bf16[384,512]{1,0:T(8,128)(2,1)S(1)}, u32[]{:S(2)}, u32[]{:S(2)}) %collective-permute-start.36) | collective-permute-done | bytes 393248 | tf_op jit(solution)/shard_map/ppermute | solution.py:871
  274.8 7.2 %collective-permute-done.38.refs_0_ = bf16[512,2048]{1,0:T(8,128)(2,1)S(1)} collective-permute-done((bf16[512,2048]{1,0:T(8,128)(2,1)S(1)}, bf16[512,2048]{1,0:T(8,128)(2,1)S(1)}, u32[]{:S(2)}, u32[]{:S(2)}) %collective-permute-start.38) | collective-permute-done | bytes 2097184 | tf_op jit(solution)/shard_map/ppermute | solution.py:871
  284.7 4.5 %collective-permute-done.37.refs_0_ = bf16[768,512]{1,0:T(8,128)(2,1)S(1)} collective-permute-done((bf16[768,512]{1,0:T(8,128)(2,1)S(1)}, bf16[768,512]{1,0:T(8,128)(2,1)S(1)}, u32[]{:S(2)}, u32[]{:S(2)}) %collective-permute-start.37) | collective-permute-done | bytes 786464 | tf_op jit(solution)/shard_map/ppermute | solution.py:871
  293.8 6.1 %collective-permute-done.32 = f32[16,1024]{1,0:T(8,128)S(1)} collective-permute-done((f32[16,1024]{1,0:T(8,128)S(1)}, f32[16,1024]{1,0:T(8,128)S(1)}, u32[]{:S(2)}, u32[]{:S(2)}) %collective-permute-start.32) | collective-permute-done | bytes 65568 | tf_op jit(solution)/shard_map/ppermute | solution.py:871
  302.7 3.3 %collective-permute-done.40 = f32[16,1024]{1,0:T(8,128)S(1)} collective-permute-done((f32[16,1024]{1,0:T(8,128)S(1)}, f32[16,1024]{1,0:T(8,128)S(1)}, u32[]{:S(2)}, u32[]{:S(2)}) %collective-permute-start.40) | collective-permute-done | bytes 65568 | tf_op jit(solution)/shard_map/ppermute | solution.py:871
  309.2 6.9 %last_back.1 = f32[512,1024]{1,0:T(8,128)} custom-call(bf16[3,512,512]{2,1,0:T(8,128)(2,1)S(1)} %get-tuple-element.259.right_ref.d0_ref, bf16[3,512,512]{2,1,0:T(8,128)(2,1)S(1)} %get-tuple-element.184.right_ref.d1_ref, bf16[1024,512]{1,0:T(8,128)(2,1)} %refs_0_.1, bf16[1024,512]{1,0:T(8,128)(2,1)} %collective-permute-done.1.wq_ref.refs_1_, ...), custom_call_target="tpu_custom_call" | custom-call | flops 1 | bytes 1 | tf_op jit(solution)/shard_map/last_back/pallas_call | solution.py:847
  (172 shorter events, 108.6 us)
Async XLA Ops:
  0.7 12.4 %collective-permute-start.1 = (bf16[1024,512]{1,0:T(8,128)(2,1)}, bf16[1024,512]{1,0:T(8,128)(2,1)}, u32[]{:S(2)}, u32[]{:S(2)}) collective-permute-start(bf16[1024,512]{1,0:T(8,128)(2,1)} %refs_0_.1), channel_id=1, source_target_pairs={{0,1},{1,0},{2,3},{3,2},{4,5},{5,4},{6,7},{7,6},{8,9},{9,8},{10,11... | collective-permute-start | bytes 3145736 | tf_op jit(solution)/shard_map/ppermute | solution.py:871
  1.2 11.9 %collective-permute-start.2 = (bf16[1024,512]{1,0:T(8,128)(2,1)}, bf16[1024,512]{1,0:T(8,128)(2,1)}, u32[]{:S(2)}, u32[]{:S(2)}) collective-permute-start(bf16[1024,512]{1,0:T(8,128)(2,1)} %refs_2_.1), channel_id=1, source_target_pairs={{0,1},{1,0},{2,3},{3,2},{4,5},{5,4},{6,7},{7,6},{8,9},{9,8},{10,11... | collective-permute-start | bytes 3145736 | tf_op jit(solution)/shard_map/ppermute | solution.py:871
  1.3 11.8 %collective-permute-start.3 = (bf16[1024,512]{1,0:T(8,128)(2,1)}, bf16[1024,512]{1,0:T(8,128)(2,1)}, u32[]{:S(2)}, u32[]{:S(2)}) collective-permute-start(bf16[1024,512]{1,0:T(8,128)(2,1)} %refs_4_.1), channel_id=1, source_target_pairs={{0,1},{1,0},{2,3},{3,2},{4,5},{5,4},{6,7},{7,6},{8,9},{9,8},{10,11... | collective-permute-start | bytes 3145736 | tf_op jit(solution)/shard_map/ppermute | solution.py:871
  13.1 32.3 %collective-permute-start.5 = (bf16[1024,2048]{1,0:T(8,128)(2,1)}, bf16[1024,2048]{1,0:T(8,128)(2,1)}, u32[]{:S(2)}, u32[]{:S(2)}) collective-permute-start(bf16[1024,2048]{1,0:T(8,128)(2,1)} %w0_ref.5), channel_id=1, source_target_pairs={{0,1},{1,0},{2,3},{3,2},{4,5},{5,4},{6,7},{7,6},{8,9},{9,8},{10,11... | collective-permute-start | bytes 12582920 | tf_op jit(solution)/shard_map/ppermute | solution.py:871
  13.3 38.0 %collective-permute-start.6 = (bf16[2048,1024]{1,0:T(8,128)(2,1)}, bf16[2048,1024]{1,0:T(8,128)(2,1)}, u32[]{:S(2)}, u32[]{:S(2)}) collective-permute-start(bf16[2048,1024]{1,0:T(8,128)(2,1)} %w_ref.4), channel_id=1, source_target_pairs={{0,1},{1,0},{2,3},{3,2},{4,5},{5,4},{6,7},{7,6},{8,9},{9,8},{10,11... | collective-permute-start | bytes 12582920 | tf_op jit(solution)/shard_map/ppermute | solution.py:871
  13.7 21.0 %collective-permute-start.4 = (bf16[512,1024]{1,0:T(8,128)(2,1)}, bf16[512,1024]{1,0:T(8,128)(2,1)}, u32[]{:S(2)}, u32[]{:S(2)}) collective-permute-start(bf16[512,1024]{1,0:T(8,128)(2,1)} %w_ref.5), channel_id=1, source_target_pairs={{0,1},{1,0},{2,3},{3,2},{4,5},{5,4},{6,7},{7,6},{8,9},{9,8},{10,11... | collective-permute-start | bytes 3145736 | tf_op jit(solution)/shard_map/ppermute | solution.py:871
  76.8 20.5 %collective-permute-start.8 = (bf16[1024,2048]{1,0:T(8,128)(2,1)}, bf16[1024,2048]{1,0:T(8,128)(2,1)S(1)}, u32[]{:S(2)}, u32[]{:S(2)}) collective-permute-start(bf16[1024,2048]{1,0:T(8,128)(2,1)} %weight_grad.10), channel_id=1, source_target_pairs={{0,1},{1,0},{2,3},{3,2},{4,5},{5,4},{6,7},{7,6},{8,9},{9,8},{10,11... | collective-permute-start | bytes 12582920 | tf_op jit(solution)/shard_map/ppermute | solution.py:871
  79.1 26.9 %collective-permute-start.10 = (bf16[1024,1024]{1,0:T(8,128)(2,1)S(1)}, bf16[1024,1024]{1,0:T(8,128)(2,1)S(1)}, u32[]{:S(2)}, u32[]{:S(2)}) collective-permute-start(bf16[1024,1024]{1,0:T(8,128)(2,1)S(1)} %weight_grad.11), channel_id=1, source_target_pairs={{0,2},{1,5},{2,0},{3,7},{4,6},{5,1},{6,4},{7,3},{8,10},{9,13},{10,... | collective-permute-start | bytes 6291464 | tf_op jit(solution)/shard_map/ppermute | solution.py:871
  101.0 17.6 %collective-permute-start.11 = (bf16[256,1024]{1,0:T(8,128)(2,1)S(1)}, bf16[256,1024]{1,0:T(8,128)(2,1)S(1)}, u32[]{:S(2)}, u32[]{:S(2)}) collective-permute-start(bf16[256,1024]{1,0:T(8,128)(2,1)S(1)} %weight_grad.14), channel_id=1, source_target_pairs={{0,8},{1,9},{2,10},{3,11},{4,12},{5,13},{6,14},{7,15},{8,0},{9,1},... | collective-permute-start | bytes 1572872 | tf_op jit(solution)/shard_map/ppermute | solution.py:871
  102.6 26.0 %collective-permute-start.12 = (bf16[512,2048]{1,0:T(8,128)(2,1)S(1)}, bf16[512,2048]{1,0:T(8,128)(2,1)S(1)}, u32[]{:S(2)}, u32[]{:S(2)}) collective-permute-start(bf16[512,2048]{1,0:T(8,128)(2,1)S(1)} %weight_grad.13), channel_id=1, source_target_pairs={{0,2},{1,5},{2,0},{3,7},{4,6},{5,1},{6,4},{7,3},{8,10},{9,13},{10,... | collective-permute-start | bytes 6291464 | tf_op jit(solution)/shard_map/ppermute | solution.py:871
  122.0 25.7 %collective-permute-start.18 = (bf16[3072,512]{1,0:T(8,128)(2,1)S(1)}, bf16[3072,512]{1,0:T(8,128)(2,1)S(1)}, u32[]{:S(2)}, u32[]{:S(2)}) collective-permute-start(bf16[3072,512]{1,0:T(8,128)(2,1)S(1)} %heads_grad.3), channel_id=1, source_target_pairs={{0,1},{1,0},{2,3},{3,2},{4,5},{5,4},{6,7},{7,6},{8,9},{9,8},{10,11... | collective-permute-start | bytes 9437192 | tf_op jit(solution)/shard_map/ppermute | solution.py:871
  129.5 15.4 %collective-permute-start.14 = (bf16[256,2048]{1,0:T(8,128)(2,1)S(1)}, bf16[256,2048]{1,0:T(8,128)(2,1)S(1)}, u32[]{:S(2)}, u32[]{:S(2)}) collective-permute-start(bf16[256,2048]{1,0:T(8,128)(2,1)S(1)} %combine.40), channel_id=1, source_target_pairs={{0,4},{1,3},{2,6},{3,1},{4,0},{5,7},{6,2},{7,5},{8,12},{9,11},{10,... | collective-permute-start | bytes 3145736 | tf_op jit(solution)/shard_map/ppermute | solution.py:871
  131.4 15.7 %collective-permute-start.13 = (bf16[128,1024]{1,0:T(8,128)(2,1)S(1)}, bf16[128,1024]{1,0:T(8,128)(2,1)S(1)}, u32[]{:S(2)}, u32[]{:S(2)}) collective-permute-start(bf16[128,1024]{1,0:T(8,128)(2,1)S(1)} %combine.39), channel_id=1, source_target_pairs={{0,24},{1,25},{2,26},{3,27},{4,28},{5,29},{6,30},{7,31},{8,16},{9,... | collective-permute-start | bytes 786440 | tf_op jit(solution)/shard_map/ppermute | solution.py:871
  135.0 28.7 %collective-permute-start.16 = (bf16[512,1024]{1,0:T(8,128)(2,1)S(1)}, bf16[512,1024]{1,0:T(8,128)(2,1)S(1)}, u32[]{:S(2)}, u32[]{:S(2)}) collective-permute-start(bf16[512,1024]{1,0:T(8,128)(2,1)S(1)} %combine.38), channel_id=1, source_target_pairs={{0,4},{1,3},{2,6},{3,1},{4,0},{5,7},{6,2},{7,5},{8,12},{9,11},{10,... | collective-permute-start | bytes 3145736 | tf_op jit(solution)/shard_map/ppermute | solution.py:871
  145.6 12.3 %collective-permute-start.17 = (bf16[128,2048]{1,0:T(8,128)(2,1)S(1)}, bf16[128,2048]{1,0:T(8,128)(2,1)S(1)}, u32[]{:S(2)}, u32[]{:S(2)}) collective-permute-start(bf16[128,2048]{1,0:T(8,128)(2,1)S(1)} %combine.41), channel_id=1, source_target_pairs={{0,8},{1,9},{2,10},{3,11},{4,12},{5,13},{6,14},{7,15},{8,0},{9,1},... | collective-permute-start | bytes 1572872 | tf_op jit(solution)/shard_map/ppermute | solution.py:871
  149.7 34.3 %collective-permute-start.24 = (bf16[1536,512]{1,0:T(8,128)(2,1)S(1)}, bf16[1536,512]{1,0:T(8,128)(2,1)S(1)}, u32[]{:S(2)}, u32[]{:S(2)}) collective-permute-start(bf16[1536,512]{1,0:T(8,128)(2,1)S(1)} %heads_grad.4), channel_id=1, source_target_pairs={{0,2},{1,5},{2,0},{3,7},{4,6},{5,1},{6,4},{7,3},{8,10},{9,13},{10,... | collective-permute-start | bytes 4718600 | tf_op jit(solution)/shard_map/ppermute | solution.py:871
  158.8 16.7 %collective-permute-start.20 = (bf16[128,2048]{1,0:T(8,128)(2,1)S(1)}, bf16[128,2048]{1,0:T(8,128)(2,1)S(1)}, u32[]{:S(2)}, u32[]{:S(2)}) collective-permute-start(bf16[128,2048]{1,0:T(8,128)(2,1)S(1)} %combine.43.refs_0_), channel_id=1, source_target_pairs={{0,24},{1,25},{2,26},{3,27},{4,28},{5,29},{6,30},{7,31},{8,16},{9,... | collective-permute-start | bytes 1572872 | tf_op jit(solution)/shard_map/ppermute | solution.py:871
  164.4 20.4 %collective-permute-start.23 = (bf16[256,1024]{1,0:T(8,128)(2,1)S(1)}, bf16[256,1024]{1,0:T(8,128)(2,1)S(1)}, u32[]{:S(2)}, u32[]{:S(2)}) collective-permute-start(bf16[256,1024]{1,0:T(8,128)(2,1)S(1)} %combine.44), channel_id=1, source_target_pairs={{0,8},{1,9},{2,10},{3,11},{4,12},{5,13},{6,14},{7,15},{8,0},{9,1},... | collective-permute-start | bytes 1572872 | tf_op jit(solution)/shard_map/ppermute | solution.py:871
  176.1 18.4 %collective-permute-start.22 = (bf16[128,2048]{1,0:T(8,128)(2,1)S(1)}, bf16[128,2048]{1,0:T(8,128)(2,1)S(1)}, u32[]{:S(2)}, u32[]{:S(2)}) collective-permute-start(bf16[128,2048]{1,0:T(8,128)(2,1)S(1)} %combine.46.refs_0_), channel_id=1, source_target_pairs={{0,8},{1,9},{2,10},{3,11},{4,12},{5,13},{6,14},{7,15},{8,0},{9,1},... | collective-permute-start | bytes 1572872 | tf_op jit(solution)/shard_map/ppermute | solution.py:871
  195.1 28.8 %collective-permute-start.25 = (bf16[256,2048]{1,0:T(8,128)(2,1)S(1)}, bf16[256,2048]{1,0:T(8,128)(2,1)S(1)}, u32[]{:S(2)}, u32[]{:S(2)}) collective-permute-start(bf16[256,2048]{1,0:T(8,128)(2,1)S(1)} %combine.50.refs_0_), channel_id=1, source_target_pairs={{0,4},{1,3},{2,6},{3,1},{4,0},{5,7},{6,2},{7,5},{8,12},{9,11},{10,... | collective-permute-start | bytes 3145736 | tf_op jit(solution)/shard_map/ppermute | solution.py:871
  196.7 21.7 %collective-permute-start.26 = (bf16[768,512]{1,0:T(8,128)(2,1)S(1)}, bf16[768,512]{1,0:T(8,128)(2,1)S(1)}, u32[]{:S(2)}, u32[]{:S(2)}) collective-permute-start(bf16[768,512]{1,0:T(8,128)(2,1)S(1)} %combine.48), channel_id=1, source_target_pairs={{0,4},{1,3},{2,6},{3,1},{4,0},{5,7},{6,2},{7,5},{8,12},{9,11},{10,... | collective-permute-start | bytes 2359304 | tf_op jit(solution)/shard_map/ppermute | solution.py:871
  197.2 38.3 %collective-permute-start.34 = (bf16[256,1024]{1,0:T(8,128)(2,1)S(1)}, bf16[256,1024]{1,0:T(8,128)(2,1)S(1)}, u32[]{:S(2)}, u32[]{:S(2)}) collective-permute-start(bf16[256,1024]{1,0:T(8,128)(2,1)S(1)} %combine.49.refs_0_), channel_id=1, source_target_pairs={{0,24},{1,25},{2,26},{3,27},{4,28},{5,29},{6,30},{7,31},{8,16},{9,... | collective-permute-start | bytes 1572872 | tf_op jit(solution)/shard_map/ppermute | solution.py:871
  219.1 14.5 %collective-permute-start.28 = (bf16[384,512]{1,0:T(8,128)(2,1)S(1)}, bf16[384,512]{1,0:T(8,128)(2,1)S(1)}, u32[]{:S(2)}, u32[]{:S(2)}) collective-permute-start(bf16[384,512]{1,0:T(8,128)(2,1)S(1)} %combine.52), channel_id=1, source_target_pairs={{0,8},{1,9},{2,10},{3,11},{4,12},{5,13},{6,14},{7,15},{8,0},{9,1},... | collective-permute-start | bytes 1179656 | tf_op jit(solution)/shard_map/ppermute | solution.py:871
  236.1 12.1 %collective-permute-start.35 = (bf16[256,1024]{1,0:T(8,128)(2,1)S(1)}, bf16[256,1024]{1,0:T(8,128)(2,1)S(1)}, u32[]{:S(2)}, u32[]{:S(2)}) collective-permute-start(bf16[256,1024]{1,0:T(8,128)(2,1)S(1)} %combine.60.refs_0_), channel_id=1, source_target_pairs={{0,8},{1,9},{2,10},{3,11},{4,12},{5,13},{6,14},{7,15},{8,0},{9,1},... | collective-permute-start | bytes 1572872 | tf_op jit(solution)/shard_map/ppermute | solution.py:871
  236.3 45.7 %collective-permute-start.38 = (bf16[512,2048]{1,0:T(8,128)(2,1)S(1)}, bf16[512,2048]{1,0:T(8,128)(2,1)S(1)}, u32[]{:S(2)}, u32[]{:S(2)}) collective-permute-start(bf16[512,2048]{1,0:T(8,128)(2,1)S(1)} %combine.53.refs_0_), channel_id=1, source_target_pairs={{0,2},{1,5},{2,0},{3,7},{4,6},{5,1},{6,4},{7,3},{8,10},{9,13},{10,... | collective-permute-start | bytes 6291464 | tf_op jit(solution)/shard_map/ppermute | solution.py:871
  237.9 21.8 %collective-permute-start.33 = (bf16[384,512]{1,0:T(8,128)(2,1)S(1)}, bf16[384,512]{1,0:T(8,128)(2,1)S(1)}, u32[]{:S(2)}, u32[]{:S(2)}) collective-permute-start(bf16[384,512]{1,0:T(8,128)(2,1)S(1)} %combine.57.refs_0_), channel_id=1, source_target_pairs={{0,24},{1,25},{2,26},{3,27},{4,28},{5,29},{6,30},{7,31},{8,16},{9,... | collective-permute-start | bytes 1179656 | tf_op jit(solution)/shard_map/ppermute | solution.py:871
  248.8 21.7 %collective-permute-start.39 = (bf16[512,1024]{1,0:T(8,128)(2,1)S(1)}, bf16[512,1024]{1,0:T(8,128)(2,1)S(1)}, u32[]{:S(2)}, u32[]{:S(2)}) collective-permute-start(bf16[512,1024]{1,0:T(8,128)(2,1)S(1)} %combine.62.refs_0_), channel_id=1, source_target_pairs={{0,4},{1,3},{2,6},{3,1},{4,0},{5,7},{6,2},{7,5},{8,12},{9,11},{10,... | collective-permute-start | bytes 3145736 | tf_op jit(solution)/shard_map/ppermute | solution.py:871
  268.7 20.5 %collective-permute-start.37 = (bf16[768,512]{1,0:T(8,128)(2,1)S(1)}, bf16[768,512]{1,0:T(8,128)(2,1)S(1)}, u32[]{:S(2)}, u32[]{:S(2)}) collective-permute-start(bf16[768,512]{1,0:T(8,128)(2,1)S(1)} %combine.66.refs_0_), channel_id=1, source_target_pairs={{0,4},{1,3},{2,6},{3,1},{4,0},{5,7},{6,2},{7,5},{8,12},{9,11},{10,... | collective-permute-start | bytes 2359304 | tf_op jit(solution)/shard_map/ppermute | solution.py:871
  271.1 46.8 %collective-permute-start.43 = (bf16[1024,1024]{1,0:T(8,128)(2,1)S(1)}, bf16[1024,1024]{1,0:T(8,128)(2,1)S(1)}, u32[]{:S(2)}, u32[]{:S(2)}) collective-permute-start(bf16[1024,1024]{1,0:T(8,128)(2,1)S(1)} %combine.68.refs_0_), channel_id=1, source_target_pairs={{0,2},{1,5},{2,0},{3,7},{4,6},{5,1},{6,4},{7,3},{8,10},{9,13},{10,... | collective-permute-start | bytes 6291464 | tf_op jit(solution)/shard_map/ppermute | solution.py:871
  289.9 32.4 %collective-permute-start.41 = (bf16[1536,512]{1,0:T(8,128)(2,1)S(1)}, bf16[1536,512]{1,0:T(8,128)(2,1)S(1)}, u32[]{:S(2)}, u32[]{:S(2)}) collective-permute-start(bf16[1536,512]{1,0:T(8,128)(2,1)S(1)} %combine.71.refs_0_.refs_1_.refs_2_), channel_id=1, source_target_pairs={{0,2},{1,5},{2,0},{3,7},{4,6},{5,1},{6,4},{7,3},{8,10},{9,13},{10,... | collective-permute-start | bytes 4718600 | tf_op jit(solution)/shard_map/ppermute | solution.py:871
  291.4 14.6 %collective-permute-start.31 = (bf16[128,1024]{1,0:T(8,128)(2,1)S(1)}, bf16[128,1024]{1,0:T(8,128)(2,1)S(1)}, u32[]{:S(2)}, u32[]{:S(2)}) collective-permute-start(bf16[128,1024]{1,0:T(8,128)(2,1)S(1)} %combine.58.refs_0_), channel_id=1, source_target_pairs={{0,24},{1,25},{2,26},{3,27},{4,28},{5,29},{6,30},{7,31},{8,16},{9,... | collective-permute-start | bytes 786440 | tf_op jit(solution)/shard_map/ppermute | solution.py:871
  306.6 14.0 %collective-permute-start.42 = (bf16[256,1024]{1,0:T(8,128)(2,1)S(1)}, bf16[256,1024]{1,0:T(8,128)(2,1)S(1)}, u32[]{:S(2)}, u32[]{:S(2)}) collective-permute-start(bf16[256,1024]{1,0:T(8,128)(2,1)S(1)} %combine.72.refs_0_), channel_id=1, source_target_pairs={{0,8},{1,9},{2,10},{3,11},{4,12},{5,13},{6,14},{7,15},{8,0},{9,1},... | collective-permute-start | bytes 1572872 | tf_op jit(solution)/shard_map/ppermute | solution.py:871
  (25 other events, 168.3 us)
where the time goes:
time: 326 us; the launch traced here: 325 us
  Pallas kernels  166 us (51%)
  waiting for transfers between devices  92.6 us (28%)
  starting transfers between devices  57.5 us (18%)
  local copies, waits for them, and re-layouts  7.18 us (2%)
    ppermute x44, waiting for transfers between devices, move(): return lax.ppermute(values, ('batch', 'mp'), pairs)  92.6 us
    ppermute x44, starting transfers between devices, move(): return lax.ppermute(values, ('batch', 'mp'), pairs)  57.5 us
    pallas_call x38, Pallas kernels, combine(): pl.pallas_call(functools.partial(combine_kernel, len(terms)), grid_spec=p...  34.5 us
    pallas_call x9, Pallas kernels, weight_grad(): pl.pallas_call(grad_kernel, grid_spec=pltpu.PrefetchScalarGridSpec(num_sc...  20.5 us
    pallas_call x2, Pallas kernels, attend_heads(): pl.pallas_call(attend_kernel, grid=(width // columns,), in_specs=[fixed((...  20.4 us
    pallas_call x2, Pallas kernels, attend_back_heads(): pl.pallas_call(attend_back_kernel, grid=(width // pair,), in_specs=[block...  18.9 us
    pallas_call x2, Pallas kernels, up(): pl.pallas_call(up_kernel, grid=(units // columns,), in_specs=[fixed((toke...  11.8 us
    pallas_call x1, Pallas kernels, turn_back(): pl.pallas_call(turn_kernel, grid=(steps + tokens // rows,), in_specs=[act...  11.3 us
  transfers between devices with their start and end apart: 44, of which 17 were waited for; matrix products, arithmetic and copies ran while one was open for 2% of the time, Pallas kernels for 45%

commit v1 on v0

--- a/solution.py
+++ b/solution.py
@@ -271,6 +271,17 @@
     return pltpu.with_memory_space_constraint(values, pltpu.HBM)
 
 
+def row_of(ref):
+    return ref[...].astype(jnp.float32).reshape(1, -1)
+
+
+def part_of(row, step, columns):
+    out = row[:, :columns]
+    for j in range(1, row.shape[1] // columns):
+        out = jnp.where(step == j, row[:, j * columns : (j + 1) * columns], out)
+    return out
+
+
 def like(shape, kind=jnp.bfloat16):
     return jax.ShapeDtypeStruct(shape, kind)
 
@@ -342,14 +353,17 @@
     return jnp.where(lanes == head, values, jnp.zeros_like(values))
 
 
-def attend_kernel(x_ref, wq_ref, wk_ref, wv_ref, b_ref, qkv_ref, context_ref, weights_ref):
-    rows = 256
+def attend_kernel(
+    x_ref, wq_ref, wk_ref, wv_ref, bq_ref, bv_ref, qkv_ref, context_ref, weights_ref
+):
+    rows = 512
     pair = 2 * HDIM
     factor = HDIM ** (-0.5) * 1.4426950408889634
     x = x_ref[...]
-    q = (dot(x, wq_ref[...]) + b_ref[0:1, :]).astype(jnp.bfloat16)
+    step = pl.program_id(0)
+    q = (dot(x, wq_ref[...]) + part_of(row_of(bq_ref), step, wq_ref.shape[1])).astype(jnp.bfloat16)
     k = dot(x, wk_ref[...]).astype(jnp.bfloat16)
-    v = (dot(x, wv_ref[...]) + b_ref[1:2, :]).astype(jnp.bfloat16)
+    v = (dot(x, wv_ref[...]) + part_of(row_of(bv_ref), step, wv_ref.shape[1])).astype(jnp.bfloat16)
     qkv_ref[0] = q
     qkv_ref[1] = k
     qkv_ref[2] = v
@@ -371,47 +385,47 @@
             context_ref[here, lanes] = total.astype(jnp.bfloat16)
 
 
-def attend_heads(x_low, w_query, w_key, w_value, biases):
+def attend_heads(x_low, w_query, w_key, w_value, b_query, b_value):
     tokens, depth = x_low.shape
     width = w_query.shape[1]
     columns = 4 * HDIM
     weight = pl.BlockSpec((depth, columns), lambda i: (0, i))
-    bias = pl.BlockSpec((biases.shape[0], columns), lambda i: (0, i))
+    bias = fixed(b_query.shape)
     return pl.pallas_call(
         attend_kernel,
         grid=(width // columns,),
-        in_specs=[fixed((tokens, depth)), weight, weight, weight, bias],
+        in_specs=[fixed((tokens, depth)), weight, weight, weight, bias, bias],
         out_specs=[
             pl.BlockSpec((3, tokens, columns), lambda i: (0, 0, i)),
             pl.BlockSpec((tokens, columns), lambda i: (0, i)),
             pl.BlockSpec((4, tokens, tokens), lambda i: (i, 0, 0)),
         ],
         out_shape=[
-            like((3, tokens, width)),
+            pltpu.HBM((3, tokens, width), jnp.bfloat16),
             like((tokens, width)),
             pltpu.HBM((width // HDIM, tokens, tokens), jnp.bfloat16),
         ],
         cost_estimate=LITTLE,
         compiler_params=room(24),
         name="attend",
-    )(x_low, w_query, w_key, w_value, biases)
+    )(x_low, w_query, w_key, w_value, b_query, b_value)
 
 
 def resid_kernel(
-    inputs_ref, c0_ref, c1_ref, w0_ref, w1_ref, rows_ref, low_ref, normed_ref, rstd_ref
+    inputs_ref, c0_ref, c1_ref, w0_ref, w1_ref, b_ref, gain_ref, bias_ref, low_ref, normed_ref, rstd_ref
 ):
     resid = (
         inputs_ref[...]
         + (dot(c0_ref[...], w0_ref[...]) + dot(c1_ref[...], w1_ref[...]))
-        + rows_ref[0:1, :]
-    )
-    mid, normed, rstd = layer_norm(resid, rows_ref[1:2, :], rows_ref[2:3, :])
+        + row_of(b_ref)
+    )
+    mid, normed, rstd = layer_norm(resid, row_of(gain_ref), row_of(bias_ref))
     low_ref[...] = mid.astype(jnp.bfloat16)
     normed_ref[...] = normed
     rstd_ref[...] = rstd
 
 
-def resid_norm(inputs, context, w_out, vectors):
+def resid_norm(inputs, context, w_out, b_out, gain, bias):
     tokens, width = inputs.shape
     part = context[0].shape[1]
     rows = 128
@@ -421,7 +435,7 @@
     return pl.pallas_call(
         resid_kernel,
         grid=(tokens // rows,),
-        in_specs=[wide, half, half, weight, weight, fixed(vectors.shape)],
+        in_specs=[wide, half, half, weight, weight] + [fixed(b_out.shape)] * 3,
         out_specs=[wide, wide, pl.BlockSpec((rows, 1), lambda i: (i, 0))],
         out_shape=[
             like((tokens, width)),
@@ -431,40 +445,51 @@
         cost_estimate=LITTLE,
         compiler_params=room(16),
         name="resid_norm",
-    )(inputs, *context, *w_out, vectors)
-
-
-def up_kernel(mid_ref, w_ref, b_ref, activ_ref, slope_ref):
+    )(inputs, *context, *w_out, b_out, gain, bias)
+
+
+def up_kernel(mid_ref, w0_ref, w1_ref, b0_ref, b1_ref, a0_ref, a1_ref, s0_ref, s1_ref):
     rows = 128
-    bias = b_ref[pl.ds(pl.program_id(0) + 2, 1), :]
-    for start in range(0, mid_ref.shape[0], rows):
-        here = slice(start, start + rows)
-        pre = dot(mid_ref[here, :], w_ref[...]) + bias
-        below = 0.5 * (1.0 + lax.erf(pre * 0.7071067811865476))
-        density = jnp.exp(-0.5 * pre * pre) * 0.3989422804014327
-        activ_ref[here, :] = (pre * below).astype(jnp.bfloat16)
-        slope_ref[here, :] = (below + pre * density).astype(jnp.bfloat16)
-
-
-def up(mid_low, w_up, biases):
+    step = pl.program_id(0)
+    steps = pl.num_programs(0) // 2
+
+    def part(w_ref, b_ref, activ_ref, slope_ref, number):
+        bias = part_of(row_of(b_ref), number, w_ref.shape[1])
+        for start in range(0, mid_ref.shape[0], rows):
+            here = slice(start, start + rows)
+            pre = dot(mid_ref[here, :], w_ref[...]) + bias
+            below = 0.5 * (1.0 + lax.erf(pre * 0.7071067811865476))
+            density = jnp.exp(-0.5 * pre * pre) * 0.3989422804014327
+            activ_ref[here, :] = (pre * below).astype(jnp.bfloat16)
+            slope_ref[here, :] = (below + pre * density).astype(jnp.bfloat16)
+
+    @pl.when(step < steps)
+    def _():
+        part(w0_ref, b0_ref, a0_ref, s0_ref, step)
+
+    @pl.when(step >= steps)
+    def _():
+        part(w1_ref, b1_ref, a1_ref, s1_ref, step - steps)
+
+
+def up(mid_low, w_up, b_up):
     tokens, width = mid_low.shape
-    units = w_up.shape[1]
-    columns = biases.shape[1]
-    out = pl.BlockSpec((tokens, columns), lambda i: (0, i))
+    units = w_up[0].shape[1]
+    columns = 512
+    steps = units // columns
+    turns = (lambda i: jnp.minimum(i, steps - 1), lambda i: jnp.maximum(i - steps, 0))
+    block = lambda rows: [pl.BlockSpec((rows, columns), lambda i, t=t: (0, t(i))) for t in turns]
+    out = block(tokens)
     return pl.pallas_call(
         up_kernel,
-        grid=(units // columns,),
-        in_specs=[
-            fixed((tokens, width)),
-            pl.BlockSpec((width, columns), lambda i: (0, i)),
-            fixed(biases.shape),
-        ],
-        out_specs=[out, out],
-        out_shape=[like((tokens, units))] * 2,
-        cost_estimate=LITTLE,
-        compiler_params=room(16),
+        grid=(2 * steps,),
+        in_specs=[fixed((tokens, width))] + block(width) + [fixed(b_up[0].shape)] * 2,
+        out_specs=out + out,
+        out_shape=[like((tokens, units))] * 4,
+        cost_estimate=LITTLE,
+        compiler_params=room(14),
         name="up",
-    )(mid_low, w_up, biases)
+    )(mid_low, *w_up, *b_up)
 
 
 def column_sum(values):
@@ -472,7 +497,7 @@
 
 
 def turn_kernel(
-    a0_ref, a1_ref, w0_ref, w1_ref, normed_ref, rows_ref, d_out_ref,
+    a0_ref, a1_ref, w0_ref, w1_ref, normed_ref, gain1_ref, bias1_ref, b_ref, gain_ref, bias_ref, d_out_ref,
     out_ref, d_second_ref, low_ref, sums_ref, acc_ref,
 ):
     step = pl.program_id(0)
@@ -493,7 +518,9 @@
 
     @pl.when(step >= sums_of)
     def _():
-        gain1, bias1, b_down, gain, bias = [rows_ref[j : j + 1, :] for j in range(1, 6)]
+        gain1, bias1, b_down, gain, bias = [
+            row_of(r) for r in (gain1_ref, bias1_ref, b_ref, gain_ref, bias_ref)
+        ]
         first = (step - sums_of) * rows
         for start in range(0, rows, 64):
             here = slice(start, start + 64)
@@ -521,7 +548,7 @@
     return pl.pallas_call(
         turn_kernel,
         grid=(steps + tokens // rows,),
-        in_specs=[act, act, weight, weight, wide, fixed(vectors.shape), wide],
+        in_specs=[act, act, weight, weight, wide] + [fixed(v.shape) for v in vectors] + [wide],
         out_specs=[wide, wide, wide, fixed((8, width))],
         out_shape=[
             like((tokens, width)),
@@ -533,7 +560,7 @@
         cost_estimate=LITTLE,
         compiler_params=room(30),
         name="turn_back",
-    )(*activ, *w_down, normed_one, vectors, d_out)
+    )(*activ, *w_down, normed_one, *vectors, d_out)
 
 
 def grad_kernel(at_ref, left_ref, right_ref, *refs):
@@ -692,7 +719,7 @@
 
 
 def mid_kernel(
-    p0_ref, p1_ref, w0_ref, w1_ref, d_second_ref, normed_ref, rstd_ref, rows_ref,
+    p0_ref, p1_ref, w0_ref, w1_ref, d_second_ref, normed_ref, rstd_ref, gain_ref,
     resid_ref, low_ref, sums_ref, acc_ref,
 ):
     step = pl.program_id(0)
@@ -713,7 +740,7 @@
 
     @pl.when(step >= sums_of)
     def _():
-        gain = rows_ref[1:2, :]
+        gain = row_of(gain_ref)
         first = (step - sums_of) * rows
         for start in range(0, rows, 64):
             here = slice(start, start + 64)
@@ -728,7 +755,7 @@
                 sums_ref[j : j + 1, :] += parts[j]
 
 
-def mid_back(d_pre, w_up, d_second, normed, rstd, vectors):
+def mid_back(d_pre, w_up, d_second, normed, rstd, gain):
     tokens, units = d_pre[0].shape
     width = w_up[0].shape[0]
     columns, rows = 512, 128
@@ -741,7 +768,7 @@
         grid=(steps + tokens // rows,),
         in_specs=[
             part, part, weight, weight, wide, wide,
-            pl.BlockSpec((rows, 1), lambda i: (jnp.maximum(i - steps, 0), 0)), fixed(vectors.shape),
+            pl.BlockSpec((rows, 1), lambda i: (jnp.maximum(i - steps, 0), 0)), fixed(gain.shape),
         ],
         out_specs=[wide, wide, fixed((8, width))],
         out_shape=[
@@ -753,7 +780,7 @@
         cost_estimate=LITTLE,
         compiler_params=room(30),
         name="mid_back",
-    )(*d_pre, *w_up, d_second, normed, rstd, vectors)
+    )(*d_pre, *w_up, d_second, normed, rstd, gain)
 
 
 def attend_back_kernel(qkv_ref, context_ref, weights_ref, low_ref, w_ref, out_ref, sums_ref):
@@ -908,10 +935,10 @@
 
 
 ORDER = (
-    "down", "pre", "up", "D", "pre", "mid", "out", "U", "O", "D", "D", "attn", "O", "O",
-    "heads", "U", "U", "attn", "small", "U", "O", "H", "H", "U", "D", "O", "small", "U",
-    "H", "D", "U", "H", "U", "O", "small", "small", "H", "O", "D", "D", "H", "H", "D",
-    "U", "H", "small", "small", "O", "last", "D", "O", "H",
+    "down", "pre", "up", "D", "pre", "mid", "out", "U", "O", "attn", "D", "D", "O", "O",
+    "heads", "U", "U", "attn", "U", "small", "O", "H", "U", "D", "O", "U", "D", "H",
+    "H", "U", "small", "H", "U", "small", "O", "O", "H", "D", "small", "D", "H", "H",
+    "D", "O", "U", "small", "small", "H", "last", "D", "O", "H",
 )
 
 
@@ -1006,28 +1033,28 @@
     at = placement()
     page = lax.axis_index("mp").reshape(1)
     line = Line()
-    split = jnp.concatenate([b_query, b_value, b_up])
     part = b_query.shape[0]
-    split = (split, line.did(swap_core(split)))
+    b_query, b_value, b_up = [(b, swap_core(b)) for b in (b_query, b_value, b_up)]
+    line.did(b_query[1], b_value[1], b_up[1])
     hidden = line.after(hidden)
-    split = [v.astype(jnp.float32).reshape(-1, part) for v in split]
-    rows = jnp.concatenate([b_out, ln1_gain, ln1_bias, b_down, ln2_gain, ln2_bias])
-    rows = rows.astype(jnp.float32).reshape(6, -1)
     x_table, y_table, hidden, d_out = [stay(v) for v in (x_table, y_table, hidden, d_out)]
     w_query, w_key, w_value = [(stay(w), stay(swap_core(w))) for w in (w_query, w_key, w_value)]
     both = (0, 1)
 
     inputs, x_low = embed(page, cell_ids, boxes, x_table, y_table, hidden)
-    attended = [attend_heads(x_low, w_query[i], w_key[i], w_value[i], split[i]) for i in both]
+    attended = [
+        attend_heads(x_low, w_query[i], w_key[i], w_value[i], b_query[i], b_value[i]) for i in both
+    ]
     qkv, context, weights = zip(*attended)
     line.did(x_low, w_query[1], w_key[1], w_value[1])
     w_out, w_up, w_down = [
         (stay(w), stay(swap_core(line.after(w)))) for w in (w_out, w_up, w_down)
     ]
-    mid_low, normed_one, rstd_one = resid_norm(inputs, context, w_out, rows)
-    activ, slope = zip(*[up(mid_low, w_up[i], split[i]) for i in both])
+    mid_low, normed_one, rstd_one = resid_norm(inputs, context, w_out, b_out, ln1_gain, ln1_bias)
+    raised = up(mid_low, w_up, b_up)
+    activ, slope = raised[:2], raised[2:]
     layer_out, d_second, second_low, second_sums = turn_back(
-        activ, w_down, normed_one, rows, d_out
+        activ, w_down, normed_one, (ln1_gain, ln1_bias, b_down, ln2_gain, ln2_bias), d_out
     )
     line.did(second_low)
     found = {"d_pre": {}, "pre sums": {}, "heads": {}, "heads sums": {}}
@@ -1054,7 +1081,7 @@
         d_pre = [found["d_pre"][i] for i in both]
         d_pre[0] = line.after(d_pre[0])
         found["d_resid"], found["resid_low"], found["mid sums"] = mid_back(
-            d_pre, w_up, d_second, normed_one, rstd_one, rows
+            d_pre, w_up, d_second, normed_one, rstd_one, ln1_gain
         )
         line.did(found["resid_low"])
         yield
@@ -1063,7 +1090,7 @@
         for i in (1, 0):
             low = line.after(found["resid_low"])
             found["heads"][i], found["heads sums"][i] = attend_back_heads(
-                qkv[i], context[i], weights[i], low, w_out[i]
+                stay(qkv[i]), context[i], stay(weights[i]), low, w_out[i]
             )
             line.did(found["heads"][i])
             yield

time: 326 us -> 315 us (0.966)
  local copies, waits for them, and re-layouts: 7.18 us -> 3.44 us
    ppermute x44 -> x46, starting transfers between devices: 57.5 us -> 54.7 us  [move(): return lax.ppermute(values, ('batch', 'mp'), pairs)]
    ppermute x44 -> x46, waiting for transfers between devices: 92.6 us -> 91.3 us  [move(): return lax.ppermute(values, ('batch', 'mp'), pairs)]
    pallas_call x2 -> x1, Pallas kernels: 11.8 us -> 11.5 us  [up(): pl.pallas_call(up_kernel, grid=(2 * steps,), in_specs=[fixed((tokens, wid...]
  transfers between devices with their start and end apart: 44 -> 46, of which waited for: 17 -> 18; matrix products, arithmetic and copies ran while one was open for 2% -> 1% of each run, Pallas kernels for 45% -> 46%
where the time goes in v1:
time: 315 us; the launch traced here: 314 us
  Pallas kernels  163 us (52%)
  waiting for transfers between devices  91.3 us (29%)
  starting transfers between devices  54.7 us (17%)
  local copies, waits for them, and re-layouts  3.44 us (1%)
    ppermute x46, waiting for transfers between devices, move(): return lax.ppermute(values, ('batch', 'mp'), pairs)  91.3 us
    ppermute x46, starting transfers between devices, move(): return lax.ppermute(values, ('batch', 'mp'), pairs)  54.7 us
    pallas_call x38, Pallas kernels, combine(): pl.pallas_call(functools.partial(combine_kernel, len(terms)), grid_spec=p...  34.5 us
    pallas_call x9, Pallas kernels, weight_grad(): pl.pallas_call(grad_kernel, grid_spec=pltpu.PrefetchScalarGridSpec(num_sc...  20.8 us
    pallas_call x2, Pallas kernels, attend_back_heads(): pl.pallas_call(attend_back_kernel, grid=(width // pair,), in_specs=[block...  19.2 us
    pallas_call x2, Pallas kernels, attend_heads(): pl.pallas_call(attend_kernel, grid=(width // columns,), in_specs=[fixed((...  18 us
    pallas_call x1, Pallas kernels, up(): pl.pallas_call(up_kernel, grid=(2 * steps,), in_specs=[fixed((tokens, wid...  11.5 us
    pallas_call x1, Pallas kernels, turn_back(): pl.pallas_call(turn_kernel, grid=(steps + tokens // rows,), in_specs=[act...  11.2 us
  transfers between devices with their start and end apart: 46, of which 18 were waited for; matrix products, arithmetic and copies ran while one was open for 1% of the time, Pallas kernels for 46%

profile of v1, /device:TPU:0, one launch (start us, length us, event | category | flops | bytes accessed | tf_op | source)
XLA Modules:
  0.0 314.1 jit_solution(6650235450504644850)
XLA Ops:
  5.9 5.9 %embed.1 = (f32[512,1024]{1,0:T(8,128)S(1)}, bf16[512,1024]{1,0:T(8,128)(2,1)S(1)}) custom-call(s32[1]{0:T(128)} %bitcast.page_ref, s32[2,512]{1,0:T(2,128)S(1)} %copy-done.2, s32[2,128,4]{2,1,0:T(8,128)S(1)} %copy.52.boxes_ref, bf16[1024,1024]{1,0:T(8,128)(2,1)} %x_ref.1, bf16[1024,1024]{1,0:T(8,128)(2,1)} %y_ref.1, bf16[512,1024]{1,0:T(8,128)(2,1)} %hidden_ref), custom_call_target="tpu_custom_call" | custom-call | flops 1 | bytes 1 | tf_op jit(solution)/shard_map/embed/pallas_call | solution.py:323
  12.8 9.0 %attend.2 = (bf16[3,512,512]{2,1,0:T(8,128)(2,1)}, bf16[512,512]{1,0:T(8,128)(2,1)S(1)}, bf16[8,512,512]{2,1,0:T(8,128)(2,1)}) custom-call(bf16[512,1024]{1,0:T(8,128)(2,1)S(1)} %get-tuple-element.216.x_ref.left_ref, bf16[1024,512]{1,0:T(8,128)(2,1)} %refs_0_.1, bf16[1024,512]{1,0:T(8,128)(2,1)} %refs_2_.1, bf16[1024,512]{1,0:T(8,128)(2,1)} %refs_4_.1, ...), custom_call_target="tpu_custom_call" | custom-call | flops 1 | bytes 1 | tf_op jit(solution)/shard_map/attend/pallas_call | solution.py:394
  21.9 9.0 %attend.3 = (bf16[3,512,512]{2,1,0:T(8,128)(2,1)}, bf16[512,512]{1,0:T(8,128)(2,1)S(1)}, bf16[8,512,512]{2,1,0:T(8,128)(2,1)}) custom-call(bf16[512,1024]{1,0:T(8,128)(2,1)S(1)} %get-tuple-element.216.x_ref.left_ref, bf16[1024,512]{1,0:T(8,128)(2,1)} %collective-permute-done.3.wq_ref.refs_1_, bf16[1024,512]{1,0:T(8,128)(2,1)} %collective-permute-done.4.wk_ref.refs_3_, ...), custom_call_target="tpu_custom_call" | custom-call | flops 1 | bytes 1 | tf_op jit(solution)/shard_map/attend/pallas_call | solution.py:394
  30.9 4.3 %resid_norm.1 = (bf16[512,1024]{1,0:T(8,128)(2,1)S(1)}, f32[512,1024]{1,0:T(8,128)S(1)}, f32[512,1]{1,0:T(8,128)S(1)}) custom-call(f32[512,1024]{1,0:T(8,128)S(1)} %get-tuple-element.143.inputs_ref, bf16[512,512]{1,0:T(8,128)(2,1)S(1)} %get-tuple-element.185.c0_ref.left_ref.context_ref, bf16[512,512]{1,0:T(8,128)(2,1)S(1)} %get-tuple-element.172.c1_ref.left_ref.context_ref, ...), custom_call_target="tpu_custom_call" | custom-call | flops 1 | bytes 1 | tf_op jit(solution)/shard_map/resid_norm/pallas_call | solution.py:435
  35.3 11.5 %up.1 = (bf16[512,2048]{1,0:T(8,128)(2,1)S(1)}, bf16[512,2048]{1,0:T(8,128)(2,1)S(1)}, bf16[512,2048]{1,0:T(8,128)(2,1)S(1)}, bf16[512,2048]{1,0:T(8,128)(2,1)S(1)}) custom-call(bf16[512,1024]{1,0:T(8,128)(2,1)S(1)} %get-tuple-element.190.mid_ref.left_ref, bf16[1024,2048]{1,0:T(8,128)(2,1)} %w0_ref.7, bf16[1024,2048]{1,0:T(8,128)(2,1)} %collective-permute-done.7.w1_ref, ...), custom_call_target="tpu_custom_call" | custom-call | flops 1 | bytes 1 | tf_op jit(solution)/shard_map/up/pallas_call | solution.py:483
  46.9 11.2 %turn_back.1 = (bf16[512,1024]{1,0:T(8,128)(2,1)}, f32[512,1024]{1,0:T(8,128)S(1)}, bf16[512,1024]{1,0:T(8,128)(2,1)S(1)}, f32[8,1024]{1,0:T(8,128)S(1)}) custom-call(bf16[512,2048]{1,0:T(8,128)(2,1)S(1)} %get-tuple-element.181.a0_ref.left_ref, bf16[512,2048]{1,0:T(8,128)(2,1)S(1)} %get-tuple-element.158.a1_ref.left_ref, bf16[2048,1024]{1,0:T(8,128)(2,1)} %w_ref.2, ...), custom_call_target="tpu_custom_call" | custom-call | flops 1 | bytes 1 | tf_op jit(solution)/shard_map/turn_back/pallas_call | solution.py:548
  58.1 3.8 %weight_grad.9 = bf16[2048,1024]{1,0:T(8,128)(2,1)S(1)} custom-call(s32[5]{0:T(128)S(1)} %stack.20.at_ref, bf16[512,2048]{1,0:T(8,128)(2,1)S(1)} %get-tuple-element.158.a1_ref.left_ref, bf16[512,1024]{1,0:T(8,128)(2,1)S(1)} %get-tuple-element.165.right_ref.low_ref), custom_call_target="tpu_custom_call" | custom-call | flops 1 | bytes 1 | tf_op jit(solution)/shard_map/weight_grad/pallas_call | solution.py:583
  62.1 5.1 %pre_back.2 = (bf16[512,2048]{1,0:T(8,128)(2,1)S(1)}, f32[1,2048]{1,0:T(1,128)S(1)}) custom-call(bf16[512,1024]{1,0:T(8,128)(2,1)S(1)} %get-tuple-element.165.right_ref.low_ref, bf16[2048,1024]{1,0:T(8,128)(2,1)} %collective-permute-done.8.w1_ref.w_ref, bf16[512,2048]{1,0:T(8,128)(2,1)S(1)} %get-tuple-element.160.slope_ref), custom_call_target="tpu_custom_call" | custom-call | flops 1 | bytes 1 | tf_op jit(solution)/shard_map/pre_back/pallas_call | solution.py:709
  67.2 5.0 %weight_grad.10 = bf16[1024,2048]{1,0:T(8,128)(2,1)} custom-call(s32[5]{0:T(128)S(1)} %stack.20.at_ref, bf16[512,1024]{1,0:T(8,128)(2,1)S(1)} %get-tuple-element.190.mid_ref.left_ref, bf16[512,2048]{1,0:T(8,128)(2,1)S(1)} %get-tuple-element.161.right_ref.p1_ref), custom_call_target="tpu_custom_call" | custom-call | flops 1 | bytes 1 | tf_op jit(solution)/shard_map/weight_grad/pallas_call | solution.py:583
  74.7 4.1 %collective-permute-start.12 = (bf16[1024,1024]{1,0:T(8,128)(2,1)S(1)}, bf16[1024,1024]{1,0:T(8,128)(2,1)S(1)}, u32[]{:S(2)}, u32[]{:S(2)}) collective-permute-start(bf16[1024,1024]{1,0:T(8,128)(2,1)S(1)} %weight_grad.11), channel_id=1, source_target_pairs={{0,2},{1,5},{2,0},{3,7},{4,6},{5,1},{6,4},{7,3},{8,10},{9,13},{10,... | collective-permute-start | bytes 6291464 | tf_op jit(solution)/shard_map/ppermute | solution.py:898
  78.7 5.1 %pre_back.3 = (bf16[512,2048]{1,0:T(8,128)(2,1)S(1)}, f32[1,2048]{1,0:T(1,128)S(1)}) custom-call(bf16[512,1024]{1,0:T(8,128)(2,1)S(1)} %get-tuple-element.165.right_ref.low_ref, bf16[2048,1024]{1,0:T(8,128)(2,1)} %w_ref.2, bf16[512,2048]{1,0:T(8,128)(2,1)S(1)} %get-tuple-element.166.slope_ref), custom_call_target="tpu_custom_call" | custom-call | flops 1 | bytes 1 | tf_op jit(solution)/shard_map/pre_back/pallas_call | solution.py:709
  83.8 9.1 %mid_back.1 = (f32[512,1024]{1,0:T(8,128)S(1)}, bf16[512,1024]{1,0:T(8,128)(2,1)S(1)}, f32[8,1024]{1,0:T(8,128)S(1)}) custom-call(bf16[512,2048]{1,0:T(8,128)(2,1)S(1)} %get-tuple-element.168.p0_ref.right_ref, bf16[512,2048]{1,0:T(8,128)(2,1)S(1)} %get-tuple-element.161.right_ref.p1_ref, bf16[1024,2048]{1,0:T(8,128)(2,1)} %w0_ref.7, ...), custom_call_target="tpu_custom_call" | custom-call | flops 1 | bytes 1 | tf_op jit(solution)/shard_map/mid_back/pallas_call | solution.py:766
  100.6 9.6 %attend_back.2 = (bf16[3,512,512]{2,1,0:T(8,128)(2,1)S(1)}, f32[8,512]{1,0:T(8,128)S(1)}) custom-call(bf16[3,512,512]{2,1,0:T(8,128)(2,1)} %get-tuple-element.173.qkv_ref, bf16[512,512]{1,0:T(8,128)(2,1)S(1)} %get-tuple-element.172.c1_ref.left_ref.context_ref, bf16[8,512,512]{2,1,0:T(8,128)(2,1)} %get-tuple-element.174.weights_ref, ...), custom_call_target="tpu_custom_call" | custom-call | flops 1 | bytes 1 | tf_op jit(solution)/shard_map/attend_back/pallas_call | solution.py:815
  120.0 5.6 %collective-permute-done.14.refs_1_ = bf16[512,2048]{1,0:T(8,128)(2,1)S(1)} collective-permute-done((bf16[512,2048]{1,0:T(8,128)(2,1)S(1)}, bf16[512,2048]{1,0:T(8,128)(2,1)S(1)}, u32[]{:S(2)}, u32[]{:S(2)}) %collective-permute-start.14) | collective-permute-done | bytes 2097184 | tf_op jit(solution)/shard_map/ppermute | solution.py:898
  128.1 3.6 %collective-permute-start.19 = (bf16[128,1024]{1,0:T(8,128)(2,1)S(1)}, bf16[128,1024]{1,0:T(8,128)(2,1)S(1)}, u32[]{:S(2)}, u32[]{:S(2)}) collective-permute-start(bf16[128,1024]{1,0:T(8,128)(2,1)S(1)} %combine.39), channel_id=1, source_target_pairs={{0,24},{1,25},{2,26},{3,27},{4,28},{5,29},{6,30},{7,31},{8,16},{9,... | collective-permute-start | bytes 786440 | tf_op jit(solution)/shard_map/ppermute | solution.py:898
  132.2 9.6 %attend_back.3 = (bf16[3,512,512]{2,1,0:T(8,128)(2,1)S(1)}, f32[8,512]{1,0:T(8,128)S(1)}) custom-call(bf16[3,512,512]{2,1,0:T(8,128)(2,1)} %get-tuple-element.155.qkv_ref, bf16[512,512]{1,0:T(8,128)(2,1)S(1)} %get-tuple-element.185.c0_ref.left_ref.context_ref, bf16[8,512,512]{2,1,0:T(8,128)(2,1)} %get-tuple-element.156.weights_ref, ...), custom_call_target="tpu_custom_call" | custom-call | flops 1 | bytes 1 | tf_op jit(solution)/shard_map/attend_back/pallas_call | solution.py:815
  148.1 6.9 %collective-permute-done.18.refs_3_ = bf16[128,2048]{1,0:T(8,128)(2,1)S(1)} collective-permute-done((bf16[128,2048]{1,0:T(8,128)(2,1)S(1)}, bf16[128,2048]{1,0:T(8,128)(2,1)S(1)}, u32[]{:S(2)}, u32[]{:S(2)}) %collective-permute-start.18) | collective-permute-done | bytes 524320 | tf_op jit(solution)/shard_map/ppermute | solution.py:898
  155.8 3.2 %collective-permute-start.21 = (bf16[128,2048]{1,0:T(8,128)(2,1)S(1)}, bf16[128,2048]{1,0:T(8,128)(2,1)S(1)}, u32[]{:S(2)}, u32[]{:S(2)}) collective-permute-start(bf16[128,2048]{1,0:T(8,128)(2,1)S(1)} %combine.43.refs_0_), channel_id=1, source_target_pairs={{0,24},{1,25},{2,26},{3,27},{4,28},{5,29},{6,30},{7,31},{8,16},{9,... | collective-permute-start | bytes 1572872 | tf_op jit(solution)/shard_map/ppermute | solution.py:898
  161.3 7.7 %collective-permute-done.22.refs_3_ = bf16[64,1024]{1,0:T(8,128)(2,1)S(1)} collective-permute-done((bf16[64,1024]{1,0:T(8,128)(2,1)S(1)}, bf16[64,1024]{1,0:T(8,128)(2,1)S(1)}, u32[]{:S(2)}, u32[]{:S(2)}) %collective-permute-start.22) | collective-permute-done | bytes 131104 | tf_op jit(solution)/shard_map/ppermute | solution.py:898
  169.7 2.9 collective-permute-done.21.refs_1_
  173.2 7.1 %collective-permute-start.26 = (bf16[128,2048]{1,0:T(8,128)(2,1)S(1)}, bf16[128,2048]{1,0:T(8,128)(2,1)S(1)}, u32[]{:S(2)}, u32[]{:S(2)}) collective-permute-start(bf16[128,2048]{1,0:T(8,128)(2,1)S(1)} %combine.46.refs_0_), channel_id=1, source_target_pairs={{0,8},{1,9},{2,10},{3,11},{4,12},{5,13},{6,14},{7,15},{8,0},{9,1},... | collective-permute-start | bytes 1572872 | tf_op jit(solution)/shard_map/ppermute | solution.py:898
  184.6 7.1 %collective-permute-done.26.refs_0_ = bf16[128,2048]{1,0:T(8,128)(2,1)S(1)} collective-permute-done((bf16[128,2048]{1,0:T(8,128)(2,1)S(1)}, bf16[128,2048]{1,0:T(8,128)(2,1)S(1)}, u32[]{:S(2)}, u32[]{:S(2)}) %collective-permute-start.26) | collective-permute-done | bytes 524320 | tf_op jit(solution)/shard_map/ppermute | solution.py:898
  194.3 3.1 %collective-permute-start.33 = (bf16[256,1024]{1,0:T(8,128)(2,1)S(1)}, bf16[256,1024]{1,0:T(8,128)(2,1)S(1)}, u32[]{:S(2)}, u32[]{:S(2)}) collective-permute-start(bf16[256,1024]{1,0:T(8,128)(2,1)S(1)} %combine.48.refs_0_), channel_id=1, source_target_pairs={{0,24},{1,25},{2,26},{3,27},{4,28},{5,29},{6,30},{7,31},{8,16},{9,... | collective-permute-start | bytes 1572872 | tf_op jit(solution)/shard_map/ppermute | solution.py:898
  198.7 16.8 %collective-permute-done.24.refs_2_ = bf16[768,512]{1,0:T(8,128)(2,1)S(1)} collective-permute-done((bf16[768,512]{1,0:T(8,128)(2,1)S(1)}, bf16[768,512]{1,0:T(8,128)(2,1)S(1)}, u32[]{:S(2)}, u32[]{:S(2)}) %collective-permute-start.24) | collective-permute-done | bytes 786464 | tf_op jit(solution)/shard_map/ppermute | solution.py:898
  233.5 3.1 %collective-permute-start.32 = (bf16[384,512]{1,0:T(8,128)(2,1)S(1)}, bf16[384,512]{1,0:T(8,128)(2,1)S(1)}, u32[]{:S(2)}, u32[]{:S(2)}) collective-permute-start(bf16[384,512]{1,0:T(8,128)(2,1)S(1)} %combine.59.refs_0_), channel_id=1, source_target_pairs={{0,24},{1,25},{2,26},{3,27},{4,28},{5,29},{6,30},{7,31},{8,16},{9,... | collective-permute-start | bytes 1179656 | tf_op jit(solution)/shard_map/ppermute | solution.py:898
  238.0 6.2 %collective-permute-done.34.refs_0_ = bf16[256,1024]{1,0:T(8,128)(2,1)S(1)} collective-permute-done((bf16[256,1024]{1,0:T(8,128)(2,1)S(1)}, bf16[256,1024]{1,0:T(8,128)(2,1)S(1)}, u32[]{:S(2)}, u32[]{:S(2)}) %collective-permute-start.34) | collective-permute-done | bytes 524320 | tf_op jit(solution)/shard_map/ppermute | solution.py:898
  246.3 9.0 %collective-permute-done.32.refs_1_ = bf16[384,512]{1,0:T(8,128)(2,1)S(1)} collective-permute-done((bf16[384,512]{1,0:T(8,128)(2,1)S(1)}, bf16[384,512]{1,0:T(8,128)(2,1)S(1)}, u32[]{:S(2)}, u32[]{:S(2)}) %collective-permute-start.32) | collective-permute-done | bytes 393248 | tf_op jit(solution)/shard_map/ppermute | solution.py:898
  256.6 7.2 %collective-permute-done.36.refs_0_ = bf16[384,512]{1,0:T(8,128)(2,1)S(1)} collective-permute-done((bf16[384,512]{1,0:T(8,128)(2,1)S(1)}, bf16[384,512]{1,0:T(8,128)(2,1)S(1)}, u32[]{:S(2)}, u32[]{:S(2)}) %collective-permute-start.36) | collective-permute-done | bytes 393248 | tf_op jit(solution)/shard_map/ppermute | solution.py:898
  271.0 5.2 %collective-permute-done.40.refs_0_ = bf16[128,1024]{1,0:T(8,128)(2,1)S(1)} collective-permute-done((bf16[128,1024]{1,0:T(8,128)(2,1)S(1)}, bf16[128,1024]{1,0:T(8,128)(2,1)S(1)}, u32[]{:S(2)}, u32[]{:S(2)}) %collective-permute-start.40) | collective-permute-done | bytes 262176 | tf_op jit(solution)/shard_map/ppermute | solution.py:898
  282.8 4.6 %collective-permute-done.42 = f32[16,1024]{1,0:T(8,128)S(1)} collective-permute-done((f32[16,1024]{1,0:T(8,128)S(1)}, f32[16,1024]{1,0:T(8,128)S(1)}, u32[]{:S(2)}, u32[]{:S(2)}) %collective-permute-start.42) | collective-permute-done | bytes 65568 | tf_op jit(solution)/shard_map/ppermute | solution.py:898
  292.7 6.9 %last_back.1 = f32[512,1024]{1,0:T(8,128)} custom-call(bf16[3,512,512]{2,1,0:T(8,128)(2,1)S(1)} %get-tuple-element.259.right_ref.d0_ref, bf16[3,512,512]{2,1,0:T(8,128)(2,1)S(1)} %get-tuple-element.180.right_ref.d1_ref, bf16[1024,512]{1,0:T(8,128)(2,1)} %refs_0_.1, bf16[1024,512]{1,0:T(8,128)(2,1)} %collective-permute-done.3.wq_ref.refs_1_, ...), custom_call_target="tpu_custom_call" | custom-call | flops 1 | bytes 1 | tf_op jit(solution)/shard_map/last_back/pallas_call | solution.py:874
  305.7 6.0 %collective-permute-done.43.refs_0_.refs_1_.refs_2_ = bf16[1536,512]{1,0:T(8,128)(2,1)S(1)} collective-permute-done((bf16[1536,512]{1,0:T(8,128)(2,1)S(1)}, bf16[1536,512]{1,0:T(8,128)(2,1)S(1)}, u32[]{:S(2)}, u32[]{:S(2)}) %collective-permute-start.43) | collective-permute-done | bytes 1572896 | tf_op jit(solution)/shard_map/ppermute | solution.py:898
  (156 shorter events, 98.1 us)
Async XLA Ops:
  0.7 11.1 %collective-permute-start.3 = (bf16[1024,512]{1,0:T(8,128)(2,1)}, bf16[1024,512]{1,0:T(8,128)(2,1)}, u32[]{:S(2)}, u32[]{:S(2)}) collective-permute-start(bf16[1024,512]{1,0:T(8,128)(2,1)} %refs_0_.1), channel_id=1, source_target_pairs={{0,1},{1,0},{2,3},{3,2},{4,5},{5,4},{6,7},{7,6},{8,9},{9,8},{10,11... | collective-permute-start | bytes 3145736 | tf_op jit(solution)/shard_map/ppermute | solution.py:898
  1.2 10.6 %collective-permute-start.4 = (bf16[1024,512]{1,0:T(8,128)(2,1)}, bf16[1024,512]{1,0:T(8,128)(2,1)}, u32[]{:S(2)}, u32[]{:S(2)}) collective-permute-start(bf16[1024,512]{1,0:T(8,128)(2,1)} %refs_2_.1), channel_id=1, source_target_pairs={{0,1},{1,0},{2,3},{3,2},{4,5},{5,4},{6,7},{7,6},{8,9},{9,8},{10,11... | collective-permute-start | bytes 3145736 | tf_op jit(solution)/shard_map/ppermute | solution.py:898
  11.8 23.4 %collective-permute-start.7 = (bf16[1024,2048]{1,0:T(8,128)(2,1)}, bf16[1024,2048]{1,0:T(8,128)(2,1)}, u32[]{:S(2)}, u32[]{:S(2)}) collective-permute-start(bf16[1024,2048]{1,0:T(8,128)(2,1)} %w0_ref.7), channel_id=1, source_target_pairs={{0,1},{1,0},{2,3},{3,2},{4,5},{5,4},{6,7},{7,6},{8,9},{9,8},{10,11... | collective-permute-start | bytes 12582920 | tf_op jit(solution)/shard_map/ppermute | solution.py:898
  12.2 34.6 %collective-permute-start.8 = (bf16[2048,1024]{1,0:T(8,128)(2,1)}, bf16[2048,1024]{1,0:T(8,128)(2,1)}, u32[]{:S(2)}, u32[]{:S(2)}) collective-permute-start(bf16[2048,1024]{1,0:T(8,128)(2,1)} %w_ref.2), channel_id=1, source_target_pairs={{0,1},{1,0},{2,3},{3,2},{4,5},{5,4},{6,7},{7,6},{8,9},{9,8},{10,11... | collective-permute-start | bytes 12582920 | tf_op jit(solution)/shard_map/ppermute | solution.py:898
  12.4 18.5 %collective-permute-start.6 = (bf16[512,1024]{1,0:T(8,128)(2,1)}, bf16[512,1024]{1,0:T(8,128)(2,1)}, u32[]{:S(2)}, u32[]{:S(2)}) collective-permute-start(bf16[512,1024]{1,0:T(8,128)(2,1)} %w_ref.3), channel_id=1, source_target_pairs={{0,1},{1,0},{2,3},{3,2},{4,5},{5,4},{6,7},{7,6},{8,9},{9,8},{10,11... | collective-permute-start | bytes 3145736 | tf_op jit(solution)/shard_map/ppermute | solution.py:898
  61.9 10.6 %collective-permute-start.9 = (bf16[2048,1024]{1,0:T(8,128)(2,1)S(1)}, bf16[2048,1024]{1,0:T(8,128)(2,1)S(1)}, u32[]{:S(2)}, u32[]{:S(2)}) collective-permute-start(bf16[2048,1024]{1,0:T(8,128)(2,1)S(1)} %weight_grad.9), channel_id=1, source_target_pairs={{0,1},{1,0},{2,3},{3,2},{4,5},{5,4},{6,7},{7,6},{8,9},{9,8},{10,11... | collective-permute-start | bytes 12582920 | tf_op jit(solution)/shard_map/ppermute | solution.py:898
  72.2 22.1 %collective-permute-start.10 = (bf16[1024,2048]{1,0:T(8,128)(2,1)}, bf16[1024,2048]{1,0:T(8,128)(2,1)S(1)}, u32[]{:S(2)}, u32[]{:S(2)}) collective-permute-start(bf16[1024,2048]{1,0:T(8,128)(2,1)} %weight_grad.10), channel_id=1, source_target_pairs={{0,1},{1,0},{2,3},{3,2},{4,5},{5,4},{6,7},{7,6},{8,9},{9,8},{10,11... | collective-permute-start | bytes 12582920 | tf_op jit(solution)/shard_map/ppermute | solution.py:898
  74.7 37.7 %collective-permute-start.12 = (bf16[1024,1024]{1,0:T(8,128)(2,1)S(1)}, bf16[1024,1024]{1,0:T(8,128)(2,1)S(1)}, u32[]{:S(2)}, u32[]{:S(2)}) collective-permute-start(bf16[1024,1024]{1,0:T(8,128)(2,1)S(1)} %weight_grad.11), channel_id=1, source_target_pairs={{0,2},{1,5},{2,0},{3,7},{4,6},{5,1},{6,4},{7,3},{8,10},{9,13},{10,... | collective-permute-start | bytes 6291464 | tf_op jit(solution)/shard_map/ppermute | solution.py:898
  97.9 16.3 %collective-permute-start.13 = (bf16[256,1024]{1,0:T(8,128)(2,1)S(1)}, bf16[256,1024]{1,0:T(8,128)(2,1)S(1)}, u32[]{:S(2)}, u32[]{:S(2)}) collective-permute-start(bf16[256,1024]{1,0:T(8,128)(2,1)S(1)} %weight_grad.14), channel_id=1, source_target_pairs={{0,8},{1,9},{2,10},{3,11},{4,12},{5,13},{6,14},{7,15},{8,0},{9,1},... | collective-permute-start | bytes 1572872 | tf_op jit(solution)/shard_map/ppermute | solution.py:898
  99.5 26.0 %collective-permute-start.14 = (bf16[512,2048]{1,0:T(8,128)(2,1)S(1)}, bf16[512,2048]{1,0:T(8,128)(2,1)S(1)}, u32[]{:S(2)}, u32[]{:S(2)}) collective-permute-start(bf16[512,2048]{1,0:T(8,128)(2,1)S(1)} %weight_grad.13), channel_id=1, source_target_pairs={{0,2},{1,5},{2,0},{3,7},{4,6},{5,1},{6,4},{7,3},{8,10},{9,13},{10,... | collective-permute-start | bytes 6291464 | tf_op jit(solution)/shard_map/ppermute | solution.py:898
  117.7 26.7 %collective-permute-start.15 = (bf16[3072,512]{1,0:T(8,128)(2,1)S(1)}, bf16[3072,512]{1,0:T(8,128)(2,1)S(1)}, u32[]{:S(2)}, u32[]{:S(2)}) collective-permute-start(bf16[3072,512]{1,0:T(8,128)(2,1)S(1)} %heads_grad.3), channel_id=1, source_target_pairs={{0,1},{1,0},{2,3},{3,2},{4,5},{5,4},{6,7},{7,6},{8,9},{9,8},{10,11... | collective-permute-start | bytes 9437192 | tf_op jit(solution)/shard_map/ppermute | solution.py:898
  126.4 15.5 %collective-permute-start.17 = (bf16[256,2048]{1,0:T(8,128)(2,1)S(1)}, bf16[256,2048]{1,0:T(8,128)(2,1)S(1)}, u32[]{:S(2)}, u32[]{:S(2)}) collective-permute-start(bf16[256,2048]{1,0:T(8,128)(2,1)S(1)} %combine.40), channel_id=1, source_target_pairs={{0,4},{1,3},{2,6},{3,1},{4,0},{5,7},{6,2},{7,5},{8,12},{9,11},{10,... | collective-permute-start | bytes 3145736 | tf_op jit(solution)/shard_map/ppermute | solution.py:898
  128.1 15.7 %collective-permute-start.19 = (bf16[128,1024]{1,0:T(8,128)(2,1)S(1)}, bf16[128,1024]{1,0:T(8,128)(2,1)S(1)}, u32[]{:S(2)}, u32[]{:S(2)}) collective-permute-start(bf16[128,1024]{1,0:T(8,128)(2,1)S(1)} %combine.39), channel_id=1, source_target_pairs={{0,24},{1,25},{2,26},{3,27},{4,28},{5,29},{6,30},{7,31},{8,16},{9,... | collective-permute-start | bytes 786440 | tf_op jit(solution)/shard_map/ppermute | solution.py:898
  131.7 28.8 %collective-permute-start.16 = (bf16[512,1024]{1,0:T(8,128)(2,1)S(1)}, bf16[512,1024]{1,0:T(8,128)(2,1)S(1)}, u32[]{:S(2)}, u32[]{:S(2)}) collective-permute-start(bf16[512,1024]{1,0:T(8,128)(2,1)S(1)} %combine.38), channel_id=1, source_target_pairs={{0,4},{1,3},{2,6},{3,1},{4,0},{5,7},{6,2},{7,5},{8,12},{9,11},{10,... | collective-permute-start | bytes 3145736 | tf_op jit(solution)/shard_map/ppermute | solution.py:898
  142.6 12.4 %collective-permute-start.18 = (bf16[128,2048]{1,0:T(8,128)(2,1)S(1)}, bf16[128,2048]{1,0:T(8,128)(2,1)S(1)}, u32[]{:S(2)}, u32[]{:S(2)}) collective-permute-start(bf16[128,2048]{1,0:T(8,128)(2,1)S(1)} %combine.41), channel_id=1, source_target_pairs={{0,8},{1,9},{2,10},{3,11},{4,12},{5,13},{6,14},{7,15},{8,0},{9,1},... | collective-permute-start | bytes 1572872 | tf_op jit(solution)/shard_map/ppermute | solution.py:898
  146.5 37.3 %collective-permute-start.23 = (bf16[1536,512]{1,0:T(8,128)(2,1)S(1)}, bf16[1536,512]{1,0:T(8,128)(2,1)S(1)}, u32[]{:S(2)}, u32[]{:S(2)}) collective-permute-start(bf16[1536,512]{1,0:T(8,128)(2,1)S(1)} %heads_grad.4), channel_id=1, source_target_pairs={{0,2},{1,5},{2,0},{3,7},{4,6},{5,1},{6,4},{7,3},{8,10},{9,13},{10,... | collective-permute-start | bytes 4718600 | tf_op jit(solution)/shard_map/ppermute | solution.py:898
  155.8 16.8 %collective-permute-start.21 = (bf16[128,2048]{1,0:T(8,128)(2,1)S(1)}, bf16[128,2048]{1,0:T(8,128)(2,1)S(1)}, u32[]{:S(2)}, u32[]{:S(2)}) collective-permute-start(bf16[128,2048]{1,0:T(8,128)(2,1)S(1)} %combine.43.refs_0_), channel_id=1, source_target_pairs={{0,24},{1,25},{2,26},{3,27},{4,28},{5,29},{6,30},{7,31},{8,16},{9,... | collective-permute-start | bytes 1572872 | tf_op jit(solution)/shard_map/ppermute | solution.py:898
  161.3 19.7 %collective-permute-start.20 = (bf16[256,1024]{1,0:T(8,128)(2,1)S(1)}, bf16[256,1024]{1,0:T(8,128)(2,1)S(1)}, u32[]{:S(2)}, u32[]{:S(2)}) collective-permute-start(bf16[256,1024]{1,0:T(8,128)(2,1)S(1)} %combine.44), channel_id=1, source_target_pairs={{0,8},{1,9},{2,10},{3,11},{4,12},{5,13},{6,14},{7,15},{8,0},{9,1},... | collective-permute-start | bytes 1572872 | tf_op jit(solution)/shard_map/ppermute | solution.py:898
  173.2 18.4 %collective-permute-start.26 = (bf16[128,2048]{1,0:T(8,128)(2,1)S(1)}, bf16[128,2048]{1,0:T(8,128)(2,1)S(1)}, u32[]{:S(2)}, u32[]{:S(2)}) collective-permute-start(bf16[128,2048]{1,0:T(8,128)(2,1)S(1)} %combine.46.refs_0_), channel_id=1, source_target_pairs={{0,8},{1,9},{2,10},{3,11},{4,12},{5,13},{6,14},{7,15},{8,0},{9,1},... | collective-permute-start | bytes 1572872 | tf_op jit(solution)/shard_map/ppermute | solution.py:898
  192.2 28.4 %collective-permute-start.30 = (bf16[256,2048]{1,0:T(8,128)(2,1)S(1)}, bf16[256,2048]{1,0:T(8,128)(2,1)S(1)}, u32[]{:S(2)}, u32[]{:S(2)}) collective-permute-start(bf16[256,2048]{1,0:T(8,128)(2,1)S(1)} %combine.50.refs_0_), channel_id=1, source_target_pairs={{0,4},{1,3},{2,6},{3,1},{4,0},{5,7},{6,2},{7,5},{8,12},{9,11},{10,... | collective-permute-start | bytes 3145736 | tf_op jit(solution)/shard_map/ppermute | solution.py:898
  193.8 21.7 %collective-permute-start.24 = (bf16[768,512]{1,0:T(8,128)(2,1)S(1)}, bf16[768,512]{1,0:T(8,128)(2,1)S(1)}, u32[]{:S(2)}, u32[]{:S(2)}) collective-permute-start(bf16[768,512]{1,0:T(8,128)(2,1)S(1)} %combine.49), channel_id=1, source_target_pairs={{0,4},{1,3},{2,6},{3,1},{4,0},{5,7},{6,2},{7,5},{8,12},{9,11},{10,... | collective-permute-start | bytes 2359304 | tf_op jit(solution)/shard_map/ppermute | solution.py:898
  194.3 37.1 %collective-permute-start.33 = (bf16[256,1024]{1,0:T(8,128)(2,1)S(1)}, bf16[256,1024]{1,0:T(8,128)(2,1)S(1)}, u32[]{:S(2)}, u32[]{:S(2)}) collective-permute-start(bf16[256,1024]{1,0:T(8,128)(2,1)S(1)} %combine.48.refs_0_), channel_id=1, source_target_pairs={{0,24},{1,25},{2,26},{3,27},{4,28},{5,29},{6,30},{7,31},{8,16},{9,... | collective-permute-start | bytes 1572872 | tf_op jit(solution)/shard_map/ppermute | solution.py:898
  216.2 14.5 %collective-permute-start.27 = (bf16[384,512]{1,0:T(8,128)(2,1)S(1)}, bf16[384,512]{1,0:T(8,128)(2,1)S(1)}, u32[]{:S(2)}, u32[]{:S(2)}) collective-permute-start(bf16[384,512]{1,0:T(8,128)(2,1)S(1)} %combine.52), channel_id=1, source_target_pairs={{0,8},{1,9},{2,10},{3,11},{4,12},{5,13},{6,14},{7,15},{8,0},{9,1},... | collective-permute-start | bytes 1179656 | tf_op jit(solution)/shard_map/ppermute | solution.py:898
  225.5 52.9 %collective-permute-start.39 = (bf16[512,2048]{1,0:T(8,128)(2,1)S(1)}, bf16[512,2048]{1,0:T(8,128)(2,1)S(1)}, u32[]{:S(2)}, u32[]{:S(2)}) collective-permute-start(bf16[512,2048]{1,0:T(8,128)(2,1)S(1)} %combine.53.refs_0_), channel_id=1, source_target_pairs={{0,2},{1,5},{2,0},{3,7},{4,6},{5,1},{6,4},{7,3},{8,10},{9,13},{10,... | collective-permute-start | bytes 6291464 | tf_op jit(solution)/shard_map/ppermute | solution.py:898
  232.2 12.1 %collective-permute-start.34 = (bf16[256,1024]{1,0:T(8,128)(2,1)S(1)}, bf16[256,1024]{1,0:T(8,128)(2,1)S(1)}, u32[]{:S(2)}, u32[]{:S(2)}) collective-permute-start(bf16[256,1024]{1,0:T(8,128)(2,1)S(1)} %combine.60.refs_0_), channel_id=1, source_target_pairs={{0,8},{1,9},{2,10},{3,11},{4,12},{5,13},{6,14},{7,15},{8,0},{9,1},... | collective-permute-start | bytes 1572872 | tf_op jit(solution)/shard_map/ppermute | solution.py:898
  233.5 21.9 %collective-permute-start.32 = (bf16[384,512]{1,0:T(8,128)(2,1)S(1)}, bf16[384,512]{1,0:T(8,128)(2,1)S(1)}, u32[]{:S(2)}, u32[]{:S(2)}) collective-permute-start(bf16[384,512]{1,0:T(8,128)(2,1)S(1)} %combine.59.refs_0_), channel_id=1, source_target_pairs={{0,24},{1,25},{2,26},{3,27},{4,28},{5,29},{6,30},{7,31},{8,16},{9,... | collective-permute-start | bytes 1179656 | tf_op jit(solution)/shard_map/ppermute | solution.py:898
  244.8 21.5 %collective-permute-start.41 = (bf16[512,1024]{1,0:T(8,128)(2,1)S(1)}, bf16[512,1024]{1,0:T(8,128)(2,1)S(1)}, u32[]{:S(2)}, u32[]{:S(2)}) collective-permute-start(bf16[512,1024]{1,0:T(8,128)(2,1)S(1)} %combine.62.refs_0_), channel_id=1, source_target_pairs={{0,4},{1,3},{2,6},{3,1},{4,0},{5,7},{6,2},{7,5},{8,12},{9,11},{10,... | collective-permute-start | bytes 3145736 | tf_op jit(solution)/shard_map/ppermute | solution.py:898
  264.4 23.0 %collective-permute-start.37 = (bf16[768,512]{1,0:T(8,128)(2,1)S(1)}, bf16[768,512]{1,0:T(8,128)(2,1)S(1)}, u32[]{:S(2)}, u32[]{:S(2)}) collective-permute-start(bf16[768,512]{1,0:T(8,128)(2,1)S(1)} %combine.66.refs_0_), channel_id=1, source_target_pairs={{0,4},{1,3},{2,6},{3,1},{4,0},{5,7},{6,2},{7,5},{8,12},{9,11},{10,... | collective-permute-start | bytes 2359304 | tf_op jit(solution)/shard_map/ppermute | solution.py:898
  266.9 34.6 %collective-permute-start.45 = (bf16[1024,1024]{1,0:T(8,128)(2,1)S(1)}, bf16[1024,1024]{1,0:T(8,128)(2,1)S(1)}, u32[]{:S(2)}, u32[]{:S(2)}) collective-permute-start(bf16[1024,1024]{1,0:T(8,128)(2,1)S(1)} %combine.68.refs_0_), channel_id=1, source_target_pairs={{0,2},{1,5},{2,0},{3,7},{4,6},{5,1},{6,4},{7,3},{8,10},{9,13},{10,... | collective-permute-start | bytes 6291464 | tf_op jit(solution)/shard_map/ppermute | solution.py:898
  268.3 12.8 %collective-permute-start.38 = (f32[16,1024]{1,0:T(8,128)S(1)}, f32[16,1024]{1,0:T(8,128)S(1)}, u32[]{:S(2)}, u32[]{:S(2)}) collective-permute-start(f32[16,1024]{1,0:T(8,128)S(1)} %add.29), channel_id=1, source_target_pairs={{0,8},{1,9},{2,10},{3,11},{4,12},{5,13},{6,14},{7,15},{8,0},{9,1},... | collective-permute-start | bytes 196616 | tf_op jit(solution)/shard_map/ppermute | solution.py:898
  288.0 23.8 %collective-permute-start.43 = (bf16[1536,512]{1,0:T(8,128)(2,1)S(1)}, bf16[1536,512]{1,0:T(8,128)(2,1)S(1)}, u32[]{:S(2)}, u32[]{:S(2)}) collective-permute-start(bf16[1536,512]{1,0:T(8,128)(2,1)S(1)} %combine.73.refs_0_.refs_1_.refs_2_), channel_id=1, source_target_pairs={{0,2},{1,5},{2,0},{3,7},{4,6},{5,1},{6,4},{7,3},{8,10},{9,13},{10,... | collective-permute-start | bytes 4718600 | tf_op jit(solution)/shard_map/ppermute | solution.py:898
  289.1 15.1 %collective-permute-start.44 = (bf16[256,1024]{1,0:T(8,128)(2,1)S(1)}, bf16[256,1024]{1,0:T(8,128)(2,1)S(1)}, u32[]{:S(2)}, u32[]{:S(2)}) collective-permute-start(bf16[256,1024]{1,0:T(8,128)(2,1)S(1)} %combine.70.refs_0_), channel_id=1, source_target_pairs={{0,8},{1,9},{2,10},{3,11},{4,12},{5,13},{6,14},{7,15},{8,0},{9,1},... | collective-permute-start | bytes 1572872 | tf_op jit(solution)/shard_map/ppermute | solution.py:898
  (24 other events, 155.9 us)

commit v2 on v1

--- a/solution.py
+++ b/solution.py
@@ -935,7 +935,7 @@
 
 
 ORDER = (
-    "down", "pre", "up", "D", "pre", "mid", "out", "U", "O", "attn", "D", "D", "O", "O",
+    "down", "pre", "up", "D", "pre", "mid", "out", "U", "O", "O", "attn", "D", "D", "O",
     "heads", "U", "U", "attn", "U", "small", "O", "H", "U", "D", "O", "U", "D", "H",
     "H", "U", "small", "H", "U", "small", "O", "O", "H", "D", "small", "D", "H", "H",
     "D", "O", "U", "small", "small", "H", "last", "D", "O", "H",
@@ -1037,7 +1037,9 @@
     b_query, b_value, b_up = [(b, swap_core(b)) for b in (b_query, b_value, b_up)]
     line.did(b_query[1], b_value[1], b_up[1])
     hidden = line.after(hidden)
-    x_table, y_table, hidden, d_out = [stay(v) for v in (x_table, y_table, hidden, d_out)]
+    x_table, y_table, hidden, d_out, cell_ids = [
+        stay(v) for v in (x_table, y_table, hidden, d_out, cell_ids)
+    ]
     w_query, w_key, w_value = [(stay(w), stay(swap_core(w))) for w in (w_query, w_key, w_value)]
     both = (0, 1)
 

time: 315 us -> 315 us (level)
  no operation moved by 1% of the time
where the time goes in v2:
time: 315 us; the launch traced here: 313 us
  Pallas kernels  163 us (52%)
  waiting for transfers between devices  91.3 us (29%)
  starting transfers between devices  54.7 us (17%)
    ppermute x46, waiting for transfers between devices, move(): return lax.ppermute(values, ('batch', 'mp'), pairs)  91.3 us
    ppermute x46, starting transfers between devices, move(): return lax.ppermute(values, ('batch', 'mp'), pairs)  54.7 us
    pallas_call x38, Pallas kernels, combine(): pl.pallas_call(functools.partial(combine_kernel, len(terms)), grid_spec=p...  34.5 us
    pallas_call x9, Pallas kernels, weight_grad(): pl.pallas_call(grad_kernel, grid_spec=pltpu.PrefetchScalarGridSpec(num_sc...  20.8 us
    pallas_call x2, Pallas kernels, attend_back_heads(): pl.pallas_call(attend_back_kernel, grid=(width // pair,), in_specs=[block...  19.2 us
    pallas_call x2, Pallas kernels, attend_heads(): pl.pallas_call(attend_kernel, grid=(width // columns,), in_specs=[fixed((...  18 us
    pallas_call x1, Pallas kernels, up(): pl.pallas_call(up_kernel, grid=(2 * steps,), in_specs=[fixed((tokens, wid...  11.5 us
    pallas_call x1, Pallas kernels, turn_back(): pl.pallas_call(turn_kernel, grid=(steps + tokens // rows,), in_specs=[act...  11.2 us
  transfers between devices with their start and end apart: 46, of which 18 were waited for; matrix products, arithmetic and copies ran while one was open for 1% of the time, Pallas kernels for 46%

profile of v2, /device:TPU:0, one launch (start us, length us, event | category | flops | bytes accessed | tf_op | source)
XLA Modules:
  0.0 313.4 jit_solution(966785329971343054)
XLA Ops:
  5.2 5.9 %embed.1 = (f32[512,1024]{1,0:T(8,128)S(1)}, bf16[512,1024]{1,0:T(8,128)(2,1)S(1)}) custom-call(s32[1]{0:T(128)} %bitcast.page_ref, s32[2,512]{1,0:T(2,128)} %cells_ref.1, s32[2,128,4]{2,1,0:T(8,128)S(1)} %copy.52.boxes_ref, bf16[1024,1024]{1,0:T(8,128)(2,1)} %x_ref.1, bf16[1024,1024]{1,0:T(8,128)(2,1)} %y_ref.1, bf16[512,1024]{1,0:T(8,128)(2,1)} %hidden_ref), custom_call_target="tpu_custom_call" | custom-call | flops 1 | bytes 1 | tf_op jit(solution)/shard_map/embed/pallas_call | solution.py:323
  12.2 9.0 %attend.2 = (bf16[3,512,512]{2,1,0:T(8,128)(2,1)}, bf16[512,512]{1,0:T(8,128)(2,1)S(1)}, bf16[8,512,512]{2,1,0:T(8,128)(2,1)}) custom-call(bf16[512,1024]{1,0:T(8,128)(2,1)S(1)} %get-tuple-element.216.x_ref.left_ref, bf16[1024,512]{1,0:T(8,128)(2,1)} %refs_0_.1, bf16[1024,512]{1,0:T(8,128)(2,1)} %refs_2_.1, bf16[1024,512]{1,0:T(8,128)(2,1)} %refs_4_.1, ...), custom_call_target="tpu_custom_call" | custom-call | flops 1 | bytes 1 | tf_op jit(solution)/shard_map/attend/pallas_call | solution.py:394
  21.2 9.0 %attend.3 = (bf16[3,512,512]{2,1,0:T(8,128)(2,1)}, bf16[512,512]{1,0:T(8,128)(2,1)S(1)}, bf16[8,512,512]{2,1,0:T(8,128)(2,1)}) custom-call(bf16[512,1024]{1,0:T(8,128)(2,1)S(1)} %get-tuple-element.216.x_ref.left_ref, bf16[1024,512]{1,0:T(8,128)(2,1)} %collective-permute-done.3.wq_ref.refs_1_, bf16[1024,512]{1,0:T(8,128)(2,1)} %collective-permute-done.4.wk_ref.refs_3_, ...), custom_call_target="tpu_custom_call" | custom-call | flops 1 | bytes 1 | tf_op jit(solution)/shard_map/attend/pallas_call | solution.py:394
  30.2 4.3 %resid_norm.1 = (bf16[512,1024]{1,0:T(8,128)(2,1)S(1)}, f32[512,1024]{1,0:T(8,128)S(1)}, f32[512,1]{1,0:T(8,128)S(1)}) custom-call(f32[512,1024]{1,0:T(8,128)S(1)} %get-tuple-element.143.inputs_ref, bf16[512,512]{1,0:T(8,128)(2,1)S(1)} %get-tuple-element.177.c0_ref.left_ref.context_ref, bf16[512,512]{1,0:T(8,128)(2,1)S(1)} %get-tuple-element.172.c1_ref.left_ref.context_ref, ...), custom_call_target="tpu_custom_call" | custom-call | flops 1 | bytes 1 | tf_op jit(solution)/shard_map/resid_norm/pallas_call | solution.py:435
  34.6 11.5 %up.1 = (bf16[512,2048]{1,0:T(8,128)(2,1)S(1)}, bf16[512,2048]{1,0:T(8,128)(2,1)S(1)}, bf16[512,2048]{1,0:T(8,128)(2,1)S(1)}, bf16[512,2048]{1,0:T(8,128)(2,1)S(1)}) custom-call(bf16[512,1024]{1,0:T(8,128)(2,1)S(1)} %get-tuple-element.190.mid_ref.left_ref, bf16[1024,2048]{1,0:T(8,128)(2,1)} %w0_ref.7, bf16[1024,2048]{1,0:T(8,128)(2,1)} %collective-permute-done.7.w1_ref, ...), custom_call_target="tpu_custom_call" | custom-call | flops 1 | bytes 1 | tf_op jit(solution)/shard_map/up/pallas_call | solution.py:483
  46.2 11.2 %turn_back.1 = (bf16[512,1024]{1,0:T(8,128)(2,1)}, f32[512,1024]{1,0:T(8,128)S(1)}, bf16[512,1024]{1,0:T(8,128)(2,1)S(1)}, f32[8,1024]{1,0:T(8,128)S(1)}) custom-call(bf16[512,2048]{1,0:T(8,128)(2,1)S(1)} %get-tuple-element.183.a0_ref.left_ref, bf16[512,2048]{1,0:T(8,128)(2,1)S(1)} %get-tuple-element.158.a1_ref.left_ref, bf16[2048,1024]{1,0:T(8,128)(2,1)} %w_ref.2, ...), custom_call_target="tpu_custom_call" | custom-call | flops 1 | bytes 1 | tf_op jit(solution)/shard_map/turn_back/pallas_call | solution.py:548
  57.4 3.8 %weight_grad.9 = bf16[2048,1024]{1,0:T(8,128)(2,1)S(1)} custom-call(s32[5]{0:T(128)S(1)} %stack.20.at_ref, bf16[512,2048]{1,0:T(8,128)(2,1)S(1)} %get-tuple-element.158.a1_ref.left_ref, bf16[512,1024]{1,0:T(8,128)(2,1)S(1)} %get-tuple-element.165.right_ref.low_ref), custom_call_target="tpu_custom_call" | custom-call | flops 1 | bytes 1 | tf_op jit(solution)/shard_map/weight_grad/pallas_call | solution.py:583
  61.4 5.1 %pre_back.2 = (bf16[512,2048]{1,0:T(8,128)(2,1)S(1)}, f32[1,2048]{1,0:T(1,128)S(1)}) custom-call(bf16[512,1024]{1,0:T(8,128)(2,1)S(1)} %get-tuple-element.165.right_ref.low_ref, bf16[2048,1024]{1,0:T(8,128)(2,1)} %collective-permute-done.8.w1_ref.w_ref, bf16[512,2048]{1,0:T(8,128)(2,1)S(1)} %get-tuple-element.160.slope_ref), custom_call_target="tpu_custom_call" | custom-call | flops 1 | bytes 1 | tf_op jit(solution)/shard_map/pre_back/pallas_call | solution.py:709
  66.5 5.0 %weight_grad.10 = bf16[1024,2048]{1,0:T(8,128)(2,1)} custom-call(s32[5]{0:T(128)S(1)} %stack.20.at_ref, bf16[512,1024]{1,0:T(8,128)(2,1)S(1)} %get-tuple-element.190.mid_ref.left_ref, bf16[512,2048]{1,0:T(8,128)(2,1)S(1)} %get-tuple-element.161.right_ref.p1_ref), custom_call_target="tpu_custom_call" | custom-call | flops 1 | bytes 1 | tf_op jit(solution)/shard_map/weight_grad/pallas_call | solution.py:583
  74.0 4.1 %collective-permute-start.13 = (bf16[1024,1024]{1,0:T(8,128)(2,1)S(1)}, bf16[1024,1024]{1,0:T(8,128)(2,1)S(1)}, u32[]{:S(2)}, u32[]{:S(2)}) collective-permute-start(bf16[1024,1024]{1,0:T(8,128)(2,1)S(1)} %weight_grad.11), channel_id=1, source_target_pairs={{0,2},{1,5},{2,0},{3,7},{4,6},{5,1},{6,4},{7,3},{8,10},{9,13},{10,... | collective-permute-start | bytes 6291464 | tf_op jit(solution)/shard_map/ppermute | solution.py:898
  78.0 5.1 %pre_back.3 = (bf16[512,2048]{1,0:T(8,128)(2,1)S(1)}, f32[1,2048]{1,0:T(1,128)S(1)}) custom-call(bf16[512,1024]{1,0:T(8,128)(2,1)S(1)} %get-tuple-element.165.right_ref.low_ref, bf16[2048,1024]{1,0:T(8,128)(2,1)} %w_ref.2, bf16[512,2048]{1,0:T(8,128)(2,1)S(1)} %get-tuple-element.166.slope_ref), custom_call_target="tpu_custom_call" | custom-call | flops 1 | bytes 1 | tf_op jit(solution)/shard_map/pre_back/pallas_call | solution.py:709
  83.1 9.1 %mid_back.1 = (f32[512,1024]{1,0:T(8,128)S(1)}, bf16[512,1024]{1,0:T(8,128)(2,1)S(1)}, f32[8,1024]{1,0:T(8,128)S(1)}) custom-call(bf16[512,2048]{1,0:T(8,128)(2,1)S(1)} %get-tuple-element.168.p0_ref.right_ref, bf16[512,2048]{1,0:T(8,128)(2,1)S(1)} %get-tuple-element.161.right_ref.p1_ref, bf16[1024,2048]{1,0:T(8,128)(2,1)} %w0_ref.7, ...), custom_call_target="tpu_custom_call" | custom-call | flops 1 | bytes 1 | tf_op jit(solution)/shard_map/mid_back/pallas_call | solution.py:766
  100.9 9.6 %attend_back.2 = (bf16[3,512,512]{2,1,0:T(8,128)(2,1)S(1)}, f32[8,512]{1,0:T(8,128)S(1)}) custom-call(bf16[3,512,512]{2,1,0:T(8,128)(2,1)} %get-tuple-element.179.qkv_ref, bf16[512,512]{1,0:T(8,128)(2,1)S(1)} %get-tuple-element.172.c1_ref.left_ref.context_ref, bf16[8,512,512]{2,1,0:T(8,128)(2,1)} %get-tuple-element.180.weights_ref, ...), custom_call_target="tpu_custom_call" | custom-call | flops 1 | bytes 1 | tf_op jit(solution)/shard_map/attend_back/pallas_call | solution.py:815
  119.3 5.6 %collective-permute-done.14.refs_1_ = bf16[512,2048]{1,0:T(8,128)(2,1)S(1)} collective-permute-done((bf16[512,2048]{1,0:T(8,128)(2,1)S(1)}, bf16[512,2048]{1,0:T(8,128)(2,1)S(1)}, u32[]{:S(2)}, u32[]{:S(2)}) %collective-permute-start.14) | collective-permute-done | bytes 2097184 | tf_op jit(solution)/shard_map/ppermute | solution.py:898
  127.4 3.6 %collective-permute-start.19 = (bf16[128,1024]{1,0:T(8,128)(2,1)S(1)}, bf16[128,1024]{1,0:T(8,128)(2,1)S(1)}, u32[]{:S(2)}, u32[]{:S(2)}) collective-permute-start(bf16[128,1024]{1,0:T(8,128)(2,1)S(1)} %combine.39), channel_id=1, source_target_pairs={{0,24},{1,25},{2,26},{3,27},{4,28},{5,29},{6,30},{7,31},{8,16},{9,... | collective-permute-start | bytes 786440 | tf_op jit(solution)/shard_map/ppermute | solution.py:898
  131.6 9.6 %attend_back.3 = (bf16[3,512,512]{2,1,0:T(8,128)(2,1)S(1)}, f32[8,512]{1,0:T(8,128)S(1)}) custom-call(bf16[3,512,512]{2,1,0:T(8,128)(2,1)} %get-tuple-element.155.qkv_ref, bf16[512,512]{1,0:T(8,128)(2,1)S(1)} %get-tuple-element.177.c0_ref.left_ref.context_ref, bf16[8,512,512]{2,1,0:T(8,128)(2,1)} %get-tuple-element.156.weights_ref, ...), custom_call_target="tpu_custom_call" | custom-call | flops 1 | bytes 1 | tf_op jit(solution)/shard_map/attend_back/pallas_call | solution.py:815
  147.3 7.0 %collective-permute-done.18.refs_3_ = bf16[128,2048]{1,0:T(8,128)(2,1)S(1)} collective-permute-done((bf16[128,2048]{1,0:T(8,128)(2,1)S(1)}, bf16[128,2048]{1,0:T(8,128)(2,1)S(1)}, u32[]{:S(2)}, u32[]{:S(2)}) %collective-permute-start.18) | collective-permute-done | bytes 524320 | tf_op jit(solution)/shard_map/ppermute | solution.py:898
  155.1 3.2 %collective-permute-start.21 = (bf16[128,2048]{1,0:T(8,128)(2,1)S(1)}, bf16[128,2048]{1,0:T(8,128)(2,1)S(1)}, u32[]{:S(2)}, u32[]{:S(2)}) collective-permute-start(bf16[128,2048]{1,0:T(8,128)(2,1)S(1)} %combine.43.refs_0_), channel_id=1, source_target_pairs={{0,24},{1,25},{2,26},{3,27},{4,28},{5,29},{6,30},{7,31},{8,16},{9,... | collective-permute-start | bytes 1572872 | tf_op jit(solution)/shard_map/ppermute | solution.py:898
  160.7 7.7 %collective-permute-done.22.refs_3_ = bf16[64,1024]{1,0:T(8,128)(2,1)S(1)} collective-permute-done((bf16[64,1024]{1,0:T(8,128)(2,1)S(1)}, bf16[64,1024]{1,0:T(8,128)(2,1)S(1)}, u32[]{:S(2)}, u32[]{:S(2)}) %collective-permute-start.22) | collective-permute-done | bytes 131104 | tf_op jit(solution)/shard_map/ppermute | solution.py:898
  169.0 2.9 collective-permute-done.21.refs_1_
  172.5 7.1 %collective-permute-start.26 = (bf16[128,2048]{1,0:T(8,128)(2,1)S(1)}, bf16[128,2048]{1,0:T(8,128)(2,1)S(1)}, u32[]{:S(2)}, u32[]{:S(2)}) collective-permute-start(bf16[128,2048]{1,0:T(8,128)(2,1)S(1)} %combine.46.refs_0_), channel_id=1, source_target_pairs={{0,8},{1,9},{2,10},{3,11},{4,12},{5,13},{6,14},{7,15},{8,0},{9,1},... | collective-permute-start | bytes 1572872 | tf_op jit(solution)/shard_map/ppermute | solution.py:898
  183.9 7.1 %collective-permute-done.26.refs_0_ = bf16[128,2048]{1,0:T(8,128)(2,1)S(1)} collective-permute-done((bf16[128,2048]{1,0:T(8,128)(2,1)S(1)}, bf16[128,2048]{1,0:T(8,128)(2,1)S(1)}, u32[]{:S(2)}, u32[]{:S(2)}) %collective-permute-start.26) | collective-permute-done | bytes 524320 | tf_op jit(solution)/shard_map/ppermute | solution.py:898
  193.6 3.1 %collective-permute-start.33 = (bf16[256,1024]{1,0:T(8,128)(2,1)S(1)}, bf16[256,1024]{1,0:T(8,128)(2,1)S(1)}, u32[]{:S(2)}, u32[]{:S(2)}) collective-permute-start(bf16[256,1024]{1,0:T(8,128)(2,1)S(1)} %combine.48.refs_0_), channel_id=1, source_target_pairs={{0,24},{1,25},{2,26},{3,27},{4,28},{5,29},{6,30},{7,31},{8,16},{9,... | collective-permute-start | bytes 1572872 | tf_op jit(solution)/shard_map/ppermute | solution.py:898
  198.1 16.8 %collective-permute-done.24.refs_2_ = bf16[768,512]{1,0:T(8,128)(2,1)S(1)} collective-permute-done((bf16[768,512]{1,0:T(8,128)(2,1)S(1)}, bf16[768,512]{1,0:T(8,128)(2,1)S(1)}, u32[]{:S(2)}, u32[]{:S(2)}) %collective-permute-start.24) | collective-permute-done | bytes 786464 | tf_op jit(solution)/shard_map/ppermute | solution.py:898
  232.8 3.1 %collective-permute-start.32 = (bf16[384,512]{1,0:T(8,128)(2,1)S(1)}, bf16[384,512]{1,0:T(8,128)(2,1)S(1)}, u32[]{:S(2)}, u32[]{:S(2)}) collective-permute-start(bf16[384,512]{1,0:T(8,128)(2,1)S(1)} %combine.59.refs_0_), channel_id=1, source_target_pairs={{0,24},{1,25},{2,26},{3,27},{4,28},{5,29},{6,30},{7,31},{8,16},{9,... | collective-permute-start | bytes 1179656 | tf_op jit(solution)/shard_map/ppermute | solution.py:898
  237.3 6.2 %collective-permute-done.34.refs_0_ = bf16[256,1024]{1,0:T(8,128)(2,1)S(1)} collective-permute-done((bf16[256,1024]{1,0:T(8,128)(2,1)S(1)}, bf16[256,1024]{1,0:T(8,128)(2,1)S(1)}, u32[]{:S(2)}, u32[]{:S(2)}) %collective-permute-start.34) | collective-permute-done | bytes 524320 | tf_op jit(solution)/shard_map/ppermute | solution.py:898
  245.6 9.0 %collective-permute-done.32.refs_1_ = bf16[384,512]{1,0:T(8,128)(2,1)S(1)} collective-permute-done((bf16[384,512]{1,0:T(8,128)(2,1)S(1)}, bf16[384,512]{1,0:T(8,128)(2,1)S(1)}, u32[]{:S(2)}, u32[]{:S(2)}) %collective-permute-start.32) | collective-permute-done | bytes 393248 | tf_op jit(solution)/shard_map/ppermute | solution.py:898
  256.0 7.2 %collective-permute-done.36.refs_0_ = bf16[384,512]{1,0:T(8,128)(2,1)S(1)} collective-permute-done((bf16[384,512]{1,0:T(8,128)(2,1)S(1)}, bf16[384,512]{1,0:T(8,128)(2,1)S(1)}, u32[]{:S(2)}, u32[]{:S(2)}) %collective-permute-start.36) | collective-permute-done | bytes 393248 | tf_op jit(solution)/shard_map/ppermute | solution.py:898
  270.3 5.3 %collective-permute-done.40.refs_0_ = bf16[128,1024]{1,0:T(8,128)(2,1)S(1)} collective-permute-done((bf16[128,1024]{1,0:T(8,128)(2,1)S(1)}, bf16[128,1024]{1,0:T(8,128)(2,1)S(1)}, u32[]{:S(2)}, u32[]{:S(2)}) %collective-permute-start.40) | collective-permute-done | bytes 262176 | tf_op jit(solution)/shard_map/ppermute | solution.py:898
  282.1 4.6 %collective-permute-done.42 = f32[16,1024]{1,0:T(8,128)S(1)} collective-permute-done((f32[16,1024]{1,0:T(8,128)S(1)}, f32[16,1024]{1,0:T(8,128)S(1)}, u32[]{:S(2)}, u32[]{:S(2)}) %collective-permute-start.42) | collective-permute-done | bytes 65568 | tf_op jit(solution)/shard_map/ppermute | solution.py:898
  292.1 6.9 %last_back.1 = f32[512,1024]{1,0:T(8,128)} custom-call(bf16[3,512,512]{2,1,0:T(8,128)(2,1)S(1)} %get-tuple-element.259.right_ref.d0_ref, bf16[3,512,512]{2,1,0:T(8,128)(2,1)S(1)} %get-tuple-element.182.right_ref.d1_ref, bf16[1024,512]{1,0:T(8,128)(2,1)} %refs_0_.1, bf16[1024,512]{1,0:T(8,128)(2,1)} %collective-permute-done.3.wq_ref.refs_1_, ...), custom_call_target="tpu_custom_call" | custom-call | flops 1 | bytes 1 | tf_op jit(solution)/shard_map/last_back/pallas_call | solution.py:874
  305.1 6.0 %collective-permute-done.43.refs_0_.refs_1_.refs_2_ = bf16[1536,512]{1,0:T(8,128)(2,1)S(1)} collective-permute-done((bf16[1536,512]{1,0:T(8,128)(2,1)S(1)}, bf16[1536,512]{1,0:T(8,128)(2,1)S(1)}, u32[]{:S(2)}, u32[]{:S(2)}) %collective-permute-start.43) | collective-permute-done | bytes 1572896 | tf_op jit(solution)/shard_map/ppermute | solution.py:898
  (154 shorter events, 97.4 us)
Async XLA Ops:
  0.7 10.5 %collective-permute-start.3 = (bf16[1024,512]{1,0:T(8,128)(2,1)}, bf16[1024,512]{1,0:T(8,128)(2,1)}, u32[]{:S(2)}, u32[]{:S(2)}) collective-permute-start(bf16[1024,512]{1,0:T(8,128)(2,1)} %refs_0_.1), channel_id=1, source_target_pairs={{0,1},{1,0},{2,3},{3,2},{4,5},{5,4},{6,7},{7,6},{8,9},{9,8},{10,11... | collective-permute-start | bytes 3145736 | tf_op jit(solution)/shard_map/ppermute | solution.py:898
  11.1 23.4 %collective-permute-start.7 = (bf16[1024,2048]{1,0:T(8,128)(2,1)}, bf16[1024,2048]{1,0:T(8,128)(2,1)}, u32[]{:S(2)}, u32[]{:S(2)}) collective-permute-start(bf16[1024,2048]{1,0:T(8,128)(2,1)} %w0_ref.7), channel_id=1, source_target_pairs={{0,1},{1,0},{2,3},{3,2},{4,5},{5,4},{6,7},{7,6},{8,9},{9,8},{10,11... | collective-permute-start | bytes 12582920 | tf_op jit(solution)/shard_map/ppermute | solution.py:898
  11.6 34.6 %collective-permute-start.8 = (bf16[2048,1024]{1,0:T(8,128)(2,1)}, bf16[2048,1024]{1,0:T(8,128)(2,1)}, u32[]{:S(2)}, u32[]{:S(2)}) collective-permute-start(bf16[2048,1024]{1,0:T(8,128)(2,1)} %w_ref.2), channel_id=1, source_target_pairs={{0,1},{1,0},{2,3},{3,2},{4,5},{5,4},{6,7},{7,6},{8,9},{9,8},{10,11... | collective-permute-start | bytes 12582920 | tf_op jit(solution)/shard_map/ppermute | solution.py:898
  11.7 18.5 %collective-permute-start.6 = (bf16[512,1024]{1,0:T(8,128)(2,1)}, bf16[512,1024]{1,0:T(8,128)(2,1)}, u32[]{:S(2)}, u32[]{:S(2)}) collective-permute-start(bf16[512,1024]{1,0:T(8,128)(2,1)} %w_ref.3), channel_id=1, source_target_pairs={{0,1},{1,0},{2,3},{3,2},{4,5},{5,4},{6,7},{7,6},{8,9},{9,8},{10,11... | collective-permute-start | bytes 3145736 | tf_op jit(solution)/shard_map/ppermute | solution.py:898
  61.2 10.6 %collective-permute-start.9 = (bf16[2048,1024]{1,0:T(8,128)(2,1)S(1)}, bf16[2048,1024]{1,0:T(8,128)(2,1)S(1)}, u32[]{:S(2)}, u32[]{:S(2)}) collective-permute-start(bf16[2048,1024]{1,0:T(8,128)(2,1)S(1)} %weight_grad.9), channel_id=1, source_target_pairs={{0,1},{1,0},{2,3},{3,2},{4,5},{5,4},{6,7},{7,6},{8,9},{9,8},{10,11... | collective-permute-start | bytes 12582920 | tf_op jit(solution)/shard_map/ppermute | solution.py:898
  71.5 22.1 %collective-permute-start.10 = (bf16[1024,2048]{1,0:T(8,128)(2,1)}, bf16[1024,2048]{1,0:T(8,128)(2,1)S(1)}, u32[]{:S(2)}, u32[]{:S(2)}) collective-permute-start(bf16[1024,2048]{1,0:T(8,128)(2,1)} %weight_grad.10), channel_id=1, source_target_pairs={{0,1},{1,0},{2,3},{3,2},{4,5},{5,4},{6,7},{7,6},{8,9},{9,8},{10,11... | collective-permute-start | bytes 12582920 | tf_op jit(solution)/shard_map/ppermute | solution.py:898
  74.0 38.8 %collective-permute-start.13 = (bf16[1024,1024]{1,0:T(8,128)(2,1)S(1)}, bf16[1024,1024]{1,0:T(8,128)(2,1)S(1)}, u32[]{:S(2)}, u32[]{:S(2)}) collective-permute-start(bf16[1024,1024]{1,0:T(8,128)(2,1)S(1)} %weight_grad.11), channel_id=1, source_target_pairs={{0,2},{1,5},{2,0},{3,7},{4,6},{5,1},{6,4},{7,3},{8,10},{9,13},{10,... | collective-permute-start | bytes 6291464 | tf_op jit(solution)/shard_map/ppermute | solution.py:898
  97.2 16.3 %collective-permute-start.12 = (bf16[256,1024]{1,0:T(8,128)(2,1)S(1)}, bf16[256,1024]{1,0:T(8,128)(2,1)S(1)}, u32[]{:S(2)}, u32[]{:S(2)}) collective-permute-start(bf16[256,1024]{1,0:T(8,128)(2,1)S(1)} %weight_grad.14), channel_id=1, source_target_pairs={{0,8},{1,9},{2,10},{3,11},{4,12},{5,13},{6,14},{7,15},{8,0},{9,1},... | collective-permute-start | bytes 1572872 | tf_op jit(solution)/shard_map/ppermute | solution.py:898
  98.8 26.0 %collective-permute-start.14 = (bf16[512,2048]{1,0:T(8,128)(2,1)S(1)}, bf16[512,2048]{1,0:T(8,128)(2,1)S(1)}, u32[]{:S(2)}, u32[]{:S(2)}) collective-permute-start(bf16[512,2048]{1,0:T(8,128)(2,1)S(1)} %weight_grad.13), channel_id=1, source_target_pairs={{0,2},{1,5},{2,0},{3,7},{4,6},{5,1},{6,4},{7,3},{8,10},{9,13},{10,... | collective-permute-start | bytes 6291464 | tf_op jit(solution)/shard_map/ppermute | solution.py:898
  117.0 26.7 %collective-permute-start.15 = (bf16[3072,512]{1,0:T(8,128)(2,1)S(1)}, bf16[3072,512]{1,0:T(8,128)(2,1)S(1)}, u32[]{:S(2)}, u32[]{:S(2)}) collective-permute-start(bf16[3072,512]{1,0:T(8,128)(2,1)S(1)} %heads_grad.3), channel_id=1, source_target_pairs={{0,1},{1,0},{2,3},{3,2},{4,5},{5,4},{6,7},{7,6},{8,9},{9,8},{10,11... | collective-permute-start | bytes 9437192 | tf_op jit(solution)/shard_map/ppermute | solution.py:898
  125.7 15.5 %collective-permute-start.17 = (bf16[256,2048]{1,0:T(8,128)(2,1)S(1)}, bf16[256,2048]{1,0:T(8,128)(2,1)S(1)}, u32[]{:S(2)}, u32[]{:S(2)}) collective-permute-start(bf16[256,2048]{1,0:T(8,128)(2,1)S(1)} %combine.40), channel_id=1, source_target_pairs={{0,4},{1,3},{2,6},{3,1},{4,0},{5,7},{6,2},{7,5},{8,12},{9,11},{10,... | collective-permute-start | bytes 3145736 | tf_op jit(solution)/shard_map/ppermute | solution.py:898
  127.4 15.7 %collective-permute-start.19 = (bf16[128,1024]{1,0:T(8,128)(2,1)S(1)}, bf16[128,1024]{1,0:T(8,128)(2,1)S(1)}, u32[]{:S(2)}, u32[]{:S(2)}) collective-permute-start(bf16[128,1024]{1,0:T(8,128)(2,1)S(1)} %combine.39), channel_id=1, source_target_pairs={{0,24},{1,25},{2,26},{3,27},{4,28},{5,29},{6,30},{7,31},{8,16},{9,... | collective-permute-start | bytes 786440 | tf_op jit(solution)/shard_map/ppermute | solution.py:898
  131.0 28.8 %collective-permute-start.16 = (bf16[512,1024]{1,0:T(8,128)(2,1)S(1)}, bf16[512,1024]{1,0:T(8,128)(2,1)S(1)}, u32[]{:S(2)}, u32[]{:S(2)}) collective-permute-start(bf16[512,1024]{1,0:T(8,128)(2,1)S(1)} %combine.38), channel_id=1, source_target_pairs={{0,4},{1,3},{2,6},{3,1},{4,0},{5,7},{6,2},{7,5},{8,12},{9,11},{10,... | collective-permute-start | bytes 3145736 | tf_op jit(solution)/shard_map/ppermute | solution.py:898
  141.9 12.4 %collective-permute-start.18 = (bf16[128,2048]{1,0:T(8,128)(2,1)S(1)}, bf16[128,2048]{1,0:T(8,128)(2,1)S(1)}, u32[]{:S(2)}, u32[]{:S(2)}) collective-permute-start(bf16[128,2048]{1,0:T(8,128)(2,1)S(1)} %combine.41), channel_id=1, source_target_pairs={{0,8},{1,9},{2,10},{3,11},{4,12},{5,13},{6,14},{7,15},{8,0},{9,1},... | collective-permute-start | bytes 1572872 | tf_op jit(solution)/shard_map/ppermute | solution.py:898
  145.8 37.3 %collective-permute-start.23 = (bf16[1536,512]{1,0:T(8,128)(2,1)S(1)}, bf16[1536,512]{1,0:T(8,128)(2,1)S(1)}, u32[]{:S(2)}, u32[]{:S(2)}) collective-permute-start(bf16[1536,512]{1,0:T(8,128)(2,1)S(1)} %heads_grad.4), channel_id=1, source_target_pairs={{0,2},{1,5},{2,0},{3,7},{4,6},{5,1},{6,4},{7,3},{8,10},{9,13},{10,... | collective-permute-start | bytes 4718600 | tf_op jit(solution)/shard_map/ppermute | solution.py:898
  155.1 16.8 %collective-permute-start.21 = (bf16[128,2048]{1,0:T(8,128)(2,1)S(1)}, bf16[128,2048]{1,0:T(8,128)(2,1)S(1)}, u32[]{:S(2)}, u32[]{:S(2)}) collective-permute-start(bf16[128,2048]{1,0:T(8,128)(2,1)S(1)} %combine.43.refs_0_), channel_id=1, source_target_pairs={{0,24},{1,25},{2,26},{3,27},{4,28},{5,29},{6,30},{7,31},{8,16},{9,... | collective-permute-start | bytes 1572872 | tf_op jit(solution)/shard_map/ppermute | solution.py:898
  158.3 10.0 %collective-permute-start.22 = (bf16[64,1024]{1,0:T(8,128)(2,1)S(1)}, bf16[64,1024]{1,0:T(8,128)(2,1)S(1)}, u32[]{:S(2)}, u32[]{:S(2)}) collective-permute-start(bf16[64,1024]{1,0:T(8,128)(2,1)S(1)} %combine.42), channel_id=1, source_target_pairs={{0,2},{1,5},{2,0},{3,7},{4,6},{5,1},{6,4},{7,3},{8,10},{9,13},{10,... | collective-permute-start | bytes 393224 | tf_op jit(solution)/shard_map/ppermute | solution.py:898
  160.6 19.7 %collective-permute-start.20 = (bf16[256,1024]{1,0:T(8,128)(2,1)S(1)}, bf16[256,1024]{1,0:T(8,128)(2,1)S(1)}, u32[]{:S(2)}, u32[]{:S(2)}) collective-permute-start(bf16[256,1024]{1,0:T(8,128)(2,1)S(1)} %combine.44), channel_id=1, source_target_pairs={{0,8},{1,9},{2,10},{3,11},{4,12},{5,13},{6,14},{7,15},{8,0},{9,1},... | collective-permute-start | bytes 1572872 | tf_op jit(solution)/shard_map/ppermute | solution.py:898
  172.5 18.4 %collective-permute-start.26 = (bf16[128,2048]{1,0:T(8,128)(2,1)S(1)}, bf16[128,2048]{1,0:T(8,128)(2,1)S(1)}, u32[]{:S(2)}, u32[]{:S(2)}) collective-permute-start(bf16[128,2048]{1,0:T(8,128)(2,1)S(1)} %combine.46.refs_0_), channel_id=1, source_target_pairs={{0,8},{1,9},{2,10},{3,11},{4,12},{5,13},{6,14},{7,15},{8,0},{9,1},... | collective-permute-start | bytes 1572872 | tf_op jit(solution)/shard_map/ppermute | solution.py:898
  191.6 28.3 %collective-permute-start.30 = (bf16[256,2048]{1,0:T(8,128)(2,1)S(1)}, bf16[256,2048]{1,0:T(8,128)(2,1)S(1)}, u32[]{:S(2)}, u32[]{:S(2)}) collective-permute-start(bf16[256,2048]{1,0:T(8,128)(2,1)S(1)} %combine.50.refs_0_), channel_id=1, source_target_pairs={{0,4},{1,3},{2,6},{3,1},{4,0},{5,7},{6,2},{7,5},{8,12},{9,11},{10,... | collective-permute-start | bytes 3145736 | tf_op jit(solution)/shard_map/ppermute | solution.py:898
  193.1 21.7 %collective-permute-start.24 = (bf16[768,512]{1,0:T(8,128)(2,1)S(1)}, bf16[768,512]{1,0:T(8,128)(2,1)S(1)}, u32[]{:S(2)}, u32[]{:S(2)}) collective-permute-start(bf16[768,512]{1,0:T(8,128)(2,1)S(1)} %combine.49), channel_id=1, source_target_pairs={{0,4},{1,3},{2,6},{3,1},{4,0},{5,7},{6,2},{7,5},{8,12},{9,11},{10,... | collective-permute-start | bytes 2359304 | tf_op jit(solution)/shard_map/ppermute | solution.py:898
  193.6 37.1 %collective-permute-start.33 = (bf16[256,1024]{1,0:T(8,128)(2,1)S(1)}, bf16[256,1024]{1,0:T(8,128)(2,1)S(1)}, u32[]{:S(2)}, u32[]{:S(2)}) collective-permute-start(bf16[256,1024]{1,0:T(8,128)(2,1)S(1)} %combine.48.refs_0_), channel_id=1, source_target_pairs={{0,24},{1,25},{2,26},{3,27},{4,28},{5,29},{6,30},{7,31},{8,16},{9,... | collective-permute-start | bytes 1572872 | tf_op jit(solution)/shard_map/ppermute | solution.py:898
  215.5 14.5 %collective-permute-start.27 = (bf16[384,512]{1,0:T(8,128)(2,1)S(1)}, bf16[384,512]{1,0:T(8,128)(2,1)S(1)}, u32[]{:S(2)}, u32[]{:S(2)}) collective-permute-start(bf16[384,512]{1,0:T(8,128)(2,1)S(1)} %combine.52), channel_id=1, source_target_pairs={{0,8},{1,9},{2,10},{3,11},{4,12},{5,13},{6,14},{7,15},{8,0},{9,1},... | collective-permute-start | bytes 1179656 | tf_op jit(solution)/shard_map/ppermute | solution.py:898
  224.8 52.9 %collective-permute-start.39 = (bf16[512,2048]{1,0:T(8,128)(2,1)S(1)}, bf16[512,2048]{1,0:T(8,128)(2,1)S(1)}, u32[]{:S(2)}, u32[]{:S(2)}) collective-permute-start(bf16[512,2048]{1,0:T(8,128)(2,1)S(1)} %combine.53.refs_0_), channel_id=1, source_target_pairs={{0,2},{1,5},{2,0},{3,7},{4,6},{5,1},{6,4},{7,3},{8,10},{9,13},{10,... | collective-permute-start | bytes 6291464 | tf_op jit(solution)/shard_map/ppermute | solution.py:898
  231.4 12.1 %collective-permute-start.34 = (bf16[256,1024]{1,0:T(8,128)(2,1)S(1)}, bf16[256,1024]{1,0:T(8,128)(2,1)S(1)}, u32[]{:S(2)}, u32[]{:S(2)}) collective-permute-start(bf16[256,1024]{1,0:T(8,128)(2,1)S(1)} %combine.60.refs_0_), channel_id=1, source_target_pairs={{0,8},{1,9},{2,10},{3,11},{4,12},{5,13},{6,14},{7,15},{8,0},{9,1},... | collective-permute-start | bytes 1572872 | tf_op jit(solution)/shard_map/ppermute | solution.py:898
  232.8 21.9 %collective-permute-start.32 = (bf16[384,512]{1,0:T(8,128)(2,1)S(1)}, bf16[384,512]{1,0:T(8,128)(2,1)S(1)}, u32[]{:S(2)}, u32[]{:S(2)}) collective-permute-start(bf16[384,512]{1,0:T(8,128)(2,1)S(1)} %combine.59.refs_0_), channel_id=1, source_target_pairs={{0,24},{1,25},{2,26},{3,27},{4,28},{5,29},{6,30},{7,31},{8,16},{9,... | collective-permute-start | bytes 1179656 | tf_op jit(solution)/shard_map/ppermute | solution.py:898
  244.1 21.4 %collective-permute-start.41 = (bf16[512,1024]{1,0:T(8,128)(2,1)S(1)}, bf16[512,1024]{1,0:T(8,128)(2,1)S(1)}, u32[]{:S(2)}, u32[]{:S(2)}) collective-permute-start(bf16[512,1024]{1,0:T(8,128)(2,1)S(1)} %combine.62.refs_0_), channel_id=1, source_target_pairs={{0,4},{1,3},{2,6},{3,1},{4,0},{5,7},{6,2},{7,5},{8,12},{9,11},{10,... | collective-permute-start | bytes 3145736 | tf_op jit(solution)/shard_map/ppermute | solution.py:898
  263.7 22.9 %collective-permute-start.37 = (bf16[768,512]{1,0:T(8,128)(2,1)S(1)}, bf16[768,512]{1,0:T(8,128)(2,1)S(1)}, u32[]{:S(2)}, u32[]{:S(2)}) collective-permute-start(bf16[768,512]{1,0:T(8,128)(2,1)S(1)} %combine.66.refs_0_), channel_id=1, source_target_pairs={{0,4},{1,3},{2,6},{3,1},{4,0},{5,7},{6,2},{7,5},{8,12},{9,11},{10,... | collective-permute-start | bytes 2359304 | tf_op jit(solution)/shard_map/ppermute | solution.py:898
  266.1 34.6 %collective-permute-start.45 = (bf16[1024,1024]{1,0:T(8,128)(2,1)S(1)}, bf16[1024,1024]{1,0:T(8,128)(2,1)S(1)}, u32[]{:S(2)}, u32[]{:S(2)}) collective-permute-start(bf16[1024,1024]{1,0:T(8,128)(2,1)S(1)} %combine.68.refs_0_), channel_id=1, source_target_pairs={{0,2},{1,5},{2,0},{3,7},{4,6},{5,1},{6,4},{7,3},{8,10},{9,13},{10,... | collective-permute-start | bytes 6291464 | tf_op jit(solution)/shard_map/ppermute | solution.py:898
  267.6 12.8 %collective-permute-start.38 = (f32[16,1024]{1,0:T(8,128)S(1)}, f32[16,1024]{1,0:T(8,128)S(1)}, u32[]{:S(2)}, u32[]{:S(2)}) collective-permute-start(f32[16,1024]{1,0:T(8,128)S(1)} %add.29), channel_id=1, source_target_pairs={{0,8},{1,9},{2,10},{3,11},{4,12},{5,13},{6,14},{7,15},{8,0},{9,1},... | collective-permute-start | bytes 196616 | tf_op jit(solution)/shard_map/ppermute | solution.py:898
  287.3 23.8 %collective-permute-start.43 = (bf16[1536,512]{1,0:T(8,128)(2,1)S(1)}, bf16[1536,512]{1,0:T(8,128)(2,1)S(1)}, u32[]{:S(2)}, u32[]{:S(2)}) collective-permute-start(bf16[1536,512]{1,0:T(8,128)(2,1)S(1)} %combine.73.refs_0_.refs_1_.refs_2_), channel_id=1, source_target_pairs={{0,2},{1,5},{2,0},{3,7},{4,6},{5,1},{6,4},{7,3},{8,10},{9,13},{10,... | collective-permute-start | bytes 4718600 | tf_op jit(solution)/shard_map/ppermute | solution.py:898
  288.4 15.1 %collective-permute-start.44 = (bf16[256,1024]{1,0:T(8,128)(2,1)S(1)}, bf16[256,1024]{1,0:T(8,128)(2,1)S(1)}, u32[]{:S(2)}, u32[]{:S(2)}) collective-permute-start(bf16[256,1024]{1,0:T(8,128)(2,1)S(1)} %combine.70.refs_0_), channel_id=1, source_target_pairs={{0,8},{1,9},{2,10},{3,11},{4,12},{5,13},{6,14},{7,15},{8,0},{9,1},... | collective-permute-start | bytes 1572872 | tf_op jit(solution)/shard_map/ppermute | solution.py:898
  (23 other events, 154.4 us)
